TPU v7x, 32 devices: a whole 2x2x4 slice. The times are simulated.
32 devices in a mesh: dp: 8 (over z, y), tensor: 4 (over x, core).
Axes of the slice: x: 2, y: 2, z: 4, core: 2. Of those that a mesh axis runs over, the one named last changes fastest.
Arguments:
- hidden: bfloat16 [5120, 1152], P(('dp', 'tensor')), may hold values from -6 to 6
- in_gain: bfloat16 [1152], P('dp'), may hold values from 0.25 to 1.75
- w_query: bfloat16 [1152, 1024], P('dp', 'tensor'), may hold values from -0.1875 to 0.1875
- w_key: bfloat16 [1152, 256], P('dp'), may hold values from -0.1875 to 0.1875
- w_value: bfloat16 [1152, 256], P('dp'), may hold values from -0.1875 to 0.1875
- query_gain: bfloat16 [256], P('dp'), may hold values from 0.25 to 1.75
- key_gain: bfloat16 [256], P('dp'), may hold values from 0.25 to 1.75
- w_output: bfloat16 [1024, 1152], P('tensor', 'dp'), may hold values from -0.1875 to 0.1875
- attn_gain: bfloat16 [1152], P('dp'), may hold values from 0.25 to 1.75
- ffn_gain: bfloat16 [1152], P('dp'), may hold values from 0.25 to 1.75
- w_gate: bfloat16 [1152, 6912], P('dp', 'tensor'), may hold values from -0.1875 to 0.1875
- w_up: bfloat16 [1152, 6912], P('dp', 'tensor'), may hold values from -0.1875 to 0.1875
- w_down: bfloat16 [6912, 1152], P('tensor', 'dp'), may hold values from -0.078125 to 0.078125
- out_gain: bfloat16 [1152], P('dp'), may hold values from 0.25 to 1.75
- cotangent: bfloat16 [5120, 1152], P(('dp', 'tensor')), may hold values from -6 to 6
- segment_ids: int32 [5120], P('dp'), may hold values from 0 to 5119, as said below
- positions: int32 [5120], P('dp'), may hold values from 0 to 1999, as said below
Outputs:
- output: bfloat16 [5120, 1152], P(('dp', 'tensor'))
- grad_hidden: float32 [5120, 1152], P(('dp', 'tensor'))
- grad_in_gain: float32 [1152], P('dp')
- grad_w_query: float32 [1152, 1024], P('dp', 'tensor')
- grad_w_key: float32 [1152, 256], P('dp')
- grad_w_value: float32 [1152, 256], P('dp')
- grad_query_gain: float32 [256], P('dp')
- grad_key_gain: float32 [256], P('dp')
- grad_w_output: float32 [1024, 1152], P('tensor', 'dp')
- grad_attn_gain: float32 [1152], P('dp')
- grad_ffn_gain: float32 [1152], P('dp')
- grad_w_gate: float32 [1152, 6912], P('dp', 'tensor')
- grad_w_up: float32 [1152, 6912], P('dp', 'tensor')
- grad_w_down: float32 [6912, 1152], P('tensor', 'dp')
- grad_out_gain: float32 [1152], P('dp')
Inputs may be any that keep to these rules, and one draw needn't show every extreme that they name: `segment_ids`: segment ids never fall along the tokens and are equal exactly within a document; a document's id is the index of its first token, except that the document holding the last token has id 5120 - 1; every document holds 200 to 2000 tokens, except that the last may be cut short by the end of the array, and one document holds exactly 2000; documents may run across the bounds of packed sequences. `positions`: the offset of each token from the first token of its document.
All inputs are finite; a program needn't handle non-finite values.
Results may differ from a plain program's by a relative error of at most 0.025.
Values may be sent and summed in bfloat16 or wider, within the bound.
A program may use at most 128 MiB of HBM per device.

v0:
```python
import jax
import jax.numpy as jnp
from jax import lax
from jax.sharding import PartitionSpec as P

HD = 256
WINDOW = 512


EPSILON = 1e-06
ROPE_BASE = 10000.0


def rms_scale(values):
    return lax.rsqrt(jnp.mean(values * values, axis=-1, keepdims=True) + EPSILON)


def apply_norm(values, gain_vec):
    return values * rms_scale(values) * gain_vec.astype(jnp.float32)


def norm_back(values, gain_vec, upstream):
    factor = rms_scale(values)
    unit_rows = values * factor
    scaled = upstream * gain_vec.astype(jnp.float32)
    grad_values = factor * (
        scaled - unit_rows * jnp.mean(scaled * unit_rows, axis=-1, keepdims=True)
    )
    return (grad_values, upstream * unit_rows)


def rotary_tables(token_pos, width):
    steps_half = jnp.arange(width // 2, dtype=jnp.float32)
    frequency = ROPE_BASE ** (-2.0 * steps_half / width)
    angles = token_pos.astype(jnp.float32)[:, None] * frequency[None, :]
    return (jnp.cos(angles), jnp.sin(angles))


def rotate(values, cosine, sine_table):
    half_width = values.shape[-1] // 2
    first_half = values[..., :half_width]
    second = values[..., half_width:]
    return jnp.concatenate(
        [first_half * cosine - second * sine_table, second * cosine + first_half * sine_table],
        axis=-1,
    )


def window_mask(seq_ids):
    length_seq = seq_ids.shape[0]
    token_index = jnp.arange(length_seq, dtype=jnp.int32)
    behind = token_index[:, None] - token_index[None, :]
    return (seq_ids[:, None] == seq_ids[None, :]) & (behind >= 0) & (behind < WINDOW)


def gelu_tanh(values):
    return jax.nn.gelu(values, approximate=True)


def contract_rows(left, right):
    return lax.dot_general(
        left, right, (((0,), (0,)), ((), ())), preferred_element_type=jnp.float32
    )


def contract_cols(left, right):
    return lax.dot_general(
        left, right, (((1,), (1,)), ((), ())), preferred_element_type=jnp.float32
    )


def local(
    hidden,
    in_gain,
    w_query,
    w_key,
    w_value,
    query_gain,
    key_gain,
    w_output,
    attn_gain,
    ffn_gain,
    w_gate,
    w_up,
    w_down,
    out_gain,
    cotangent,
    segment_ids,
    positions,
):
    factor = HD ** (-0.5)
    attn_full = (
        lax.all_gather(in_gain, "dp", axis=0, tiled=True),
        lax.all_gather(w_query, "dp", axis=0, tiled=True),
        lax.all_gather(w_key, "dp", axis=0, tiled=True),
        lax.all_gather(w_value, "dp", axis=0, tiled=True),
        lax.all_gather(query_gain, "dp", axis=0, tiled=True),
        lax.all_gather(key_gain, "dp", axis=0, tiled=True),
        lax.all_gather(w_output, "dp", axis=1, tiled=True),
        lax.all_gather(attn_gain, "dp", axis=0, tiled=True),
    )
    (
        full_in_gain,
        full_query,
        full_key,
        full_value,
        full_qgain,
        full_kgain,
        full_output,
        full_attn_gain,
    ) = attn_full
    heads_local = full_query.shape[1] // HD
    hidden_f = hidden.astype(jnp.float32)
    normed_local = apply_norm(hidden_f, full_in_gain).astype(jnp.bfloat16)
    normed_in = lax.all_gather(normed_local, "tensor", axis=0, tiled=True)
    seq_len = normed_in.shape[0]
    query_raw = jnp.dot(normed_in, full_query, preferred_element_type=jnp.float32).reshape(
        seq_len, heads_local, HD
    )
    key_raw = jnp.dot(normed_in, full_key, preferred_element_type=jnp.float32)
    value_rows = jnp.dot(normed_in, full_value, preferred_element_type=jnp.float32).astype(
        jnp.bfloat16
    )
    cosine, sine_table = rotary_tables(positions, HD)
    query_rot = rotate(
        apply_norm(query_raw, full_qgain), cosine[:, None, :], sine_table[:, None, :]
    ).astype(jnp.bfloat16)
    key_rot = rotate(apply_norm(key_raw, full_kgain), cosine, sine_table).astype(jnp.bfloat16)
    allowed = window_mask(segment_ids)[None]
    scores = (
        jnp.einsum("qhd,kd->hqk", query_rot, key_rot, preferred_element_type=jnp.float32) * factor
    )
    log_total = jnp.log(jnp.sum(jnp.where(allowed, jnp.exp(scores), 0.0), axis=-1, keepdims=True))
    probs_low = jnp.where(allowed, jnp.exp(scores - log_total), 0.0).astype(jnp.bfloat16)
    context = jnp.einsum("hqk,kd->qhd", probs_low, value_rows, preferred_element_type=jnp.float32)
    context = context.reshape(seq_len, heads_local * HD).astype(jnp.bfloat16)
    attn_part = jnp.dot(context, full_output, preferred_element_type=jnp.float32)
    attn_rows = lax.psum_scatter(
        attn_part.astype(jnp.bfloat16), "tensor", scatter_dimension=0, tiled=True
    ).astype(jnp.float32)
    residual = hidden_f + apply_norm(attn_rows, full_attn_gain)
    mlp_full = (
        lax.all_gather(ffn_gain, "dp", axis=0, tiled=True),
        lax.all_gather(w_gate, "dp", axis=0, tiled=True),
        lax.all_gather(w_up, "dp", axis=0, tiled=True),
        lax.all_gather(w_down, "dp", axis=1, tiled=True),
        lax.all_gather(out_gain, "dp", axis=0, tiled=True),
    )
    full_ffn_gain, full_gate, full_up, full_down, full_out_gain = mlp_full
    ffn_local = apply_norm(residual, full_ffn_gain).astype(jnp.bfloat16)
    ffn_in = lax.all_gather(ffn_local, "tensor", axis=0, tiled=True)
    gate_pre = jnp.dot(ffn_in, full_gate, preferred_element_type=jnp.float32)
    up_pre = jnp.dot(ffn_in, full_up, preferred_element_type=jnp.float32)
    gelu_values, gelu_back = jax.vjp(gelu_tanh, gate_pre)
    mixed = (gelu_values * up_pre).astype(jnp.bfloat16)
    down_part = jnp.dot(mixed, full_down, preferred_element_type=jnp.float32)
    down_rows = lax.psum_scatter(
        down_part.astype(jnp.bfloat16), "tensor", scatter_dimension=0, tiled=True
    ).astype(jnp.float32)
    output = (residual + apply_norm(down_rows, full_out_gain)).astype(jnp.bfloat16)
    regathered = (
        lax.all_gather(in_gain, "dp", axis=0, tiled=True),
        lax.all_gather(w_query, "dp", axis=0, tiled=True),
        lax.all_gather(w_key, "dp", axis=0, tiled=True),
        lax.all_gather(w_value, "dp", axis=0, tiled=True),
        lax.all_gather(query_gain, "dp", axis=0, tiled=True),
        lax.all_gather(key_gain, "dp", axis=0, tiled=True),
        lax.all_gather(w_output, "dp", axis=1, tiled=True),
        lax.all_gather(attn_gain, "dp", axis=0, tiled=True),
        lax.all_gather(ffn_gain, "dp", axis=0, tiled=True),
        lax.all_gather(w_gate, "dp", axis=0, tiled=True),
        lax.all_gather(w_up, "dp", axis=0, tiled=True),
        lax.all_gather(w_down, "dp", axis=1, tiled=True),
        lax.all_gather(out_gain, "dp", axis=0, tiled=True),
    )
    (
        full_in_gain,
        full_query,
        full_key,
        full_value,
        full_qgain,
        full_kgain,
        full_output,
        full_attn_gain,
        full_ffn_gain,
        full_gate,
        full_up,
        full_down,
        full_out_gain,
    ) = regathered
    cot_f = cotangent.astype(jnp.float32)
    grad_down, term_out = norm_back(down_rows, full_out_gain, cot_f)
    down_all = lax.all_gather(grad_down.astype(jnp.bfloat16), "tensor", axis=0, tiled=True)
    grad_wd = contract_rows(mixed, down_all)
    grad_mixed = contract_cols(down_all, full_down)
    gate_low = gelu_back(grad_mixed * up_pre)[0].astype(jnp.bfloat16)
    up_low = (grad_mixed * gelu_values).astype(jnp.bfloat16)
    grad_wg = contract_rows(ffn_in, gate_low)
    grad_wu = contract_rows(ffn_in, up_low)
    ffn_part = contract_cols(gate_low, full_gate) + contract_cols(up_low, full_up)
    ffn_back = lax.psum_scatter(
        ffn_part.astype(jnp.bfloat16), "tensor", scatter_dimension=0, tiled=True
    ).astype(jnp.float32)
    resid_norm, term_ffn = norm_back(residual, full_ffn_gain, ffn_back)
    grad_residual = cot_f + resid_norm
    grad_attn, term_attn = norm_back(attn_rows, full_attn_gain, grad_residual)
    attn_all = lax.all_gather(grad_attn.astype(jnp.bfloat16), "tensor", axis=0, tiled=True)
    grad_wo = contract_rows(context, attn_all)
    grad_context = (
        contract_cols(attn_all, full_output).astype(jnp.bfloat16).reshape(seq_len, heads_local, HD)
    )
    scores_again = (
        jnp.einsum("qhd,kd->hqk", query_rot, key_rot, preferred_element_type=jnp.float32) * factor
    )
    probs = jnp.where(allowed, jnp.exp(scores_again - log_total), 0.0)
    grad_probs = jnp.einsum(
        "qhd,kd->hqk", grad_context, value_rows, preferred_element_type=jnp.float32
    )
    delta = jnp.sum(probs * grad_probs, axis=-1, keepdims=True)
    grad_scores = (probs * (grad_probs - delta) * factor).astype(jnp.bfloat16)
    value_heads = jnp.einsum(
        "hqk,qhd->khd", probs.astype(jnp.bfloat16), grad_context, preferred_element_type=jnp.float32
    ).astype(jnp.bfloat16)
    grad_qrot = jnp.einsum("hqk,kd->qhd", grad_scores, key_rot, preferred_element_type=jnp.float32)
    grad_kheads = jnp.einsum(
        "hqk,qhd->khd", grad_scores, query_rot, preferred_element_type=jnp.float32
    )
    grad_qraw, term_qgain = norm_back(
        query_raw, full_qgain, rotate(grad_qrot, cosine[:, None, :], -sine_table[:, None, :])
    )
    grad_kraw, term_kgain = norm_back(
        key_raw[:, None, :],
        full_kgain,
        rotate(grad_kheads, cosine[:, None, :], -sine_table[:, None, :]),
    )
    query_low = grad_qraw.astype(jnp.bfloat16).reshape(seq_len, heads_local * HD)
    key_low = grad_kraw.astype(jnp.bfloat16)
    grad_wq = contract_rows(normed_in, query_low)
    grad_wk = jnp.einsum("sd,she->de", normed_in, key_low, preferred_element_type=jnp.float32)
    grad_wv = jnp.einsum("sd,she->de", normed_in, value_heads, preferred_element_type=jnp.float32)
    attn_in_part = contract_cols(query_low, full_query)
    attn_in_part = attn_in_part + jnp.einsum(
        "she,de->sd", key_low, full_key, preferred_element_type=jnp.float32
    )
    attn_in_part = attn_in_part + jnp.einsum(
        "she,de->sd", value_heads, full_value, preferred_element_type=jnp.float32
    )
    attn_back = lax.psum_scatter(
        attn_in_part.astype(jnp.bfloat16), "tensor", scatter_dimension=0, tiled=True
    ).astype(jnp.float32)
    in_norm, term_in = norm_back(hidden_f, full_in_gain, attn_back)
    grad_hidden = grad_residual + in_norm
    shards = (
        lax.psum_scatter(
            jnp.sum(term_in, axis=0).astype(jnp.bfloat16), "dp", scatter_dimension=0, tiled=True
        ).astype(jnp.float32),
        lax.psum_scatter(
            grad_wq.astype(jnp.bfloat16), "dp", scatter_dimension=0, tiled=True
        ).astype(jnp.float32),
        lax.psum_scatter(
            grad_wk.astype(jnp.bfloat16), "dp", scatter_dimension=0, tiled=True
        ).astype(jnp.float32),
        lax.psum_scatter(
            grad_wv.astype(jnp.bfloat16), "dp", scatter_dimension=0, tiled=True
        ).astype(jnp.float32),
        lax.psum_scatter(
            jnp.sum(term_qgain, axis=(0, 1)).astype(jnp.bfloat16),
            "dp",
            scatter_dimension=0,
            tiled=True,
        ).astype(jnp.float32),
        lax.psum_scatter(
            jnp.sum(term_kgain, axis=(0, 1)).astype(jnp.bfloat16),
            "dp",
            scatter_dimension=0,
            tiled=True,
        ).astype(jnp.float32),
        lax.psum_scatter(
            grad_wo.astype(jnp.bfloat16), "dp", scatter_dimension=1, tiled=True
        ).astype(jnp.float32),
        lax.psum_scatter(
            jnp.sum(term_attn, axis=0).astype(jnp.bfloat16), "dp", scatter_dimension=0, tiled=True
        ).astype(jnp.float32),
        lax.psum_scatter(
            jnp.sum(term_ffn, axis=0).astype(jnp.bfloat16), "dp", scatter_dimension=0, tiled=True
        ).astype(jnp.float32),
        lax.psum_scatter(
            grad_wg.astype(jnp.bfloat16), "dp", scatter_dimension=0, tiled=True
        ).astype(jnp.float32),
        lax.psum_scatter(
            grad_wu.astype(jnp.bfloat16), "dp", scatter_dimension=0, tiled=True
        ).astype(jnp.float32),
        lax.psum_scatter(
            grad_wd.astype(jnp.bfloat16), "dp", scatter_dimension=1, tiled=True
        ).astype(jnp.float32),
        lax.psum_scatter(
            jnp.sum(term_out, axis=0).astype(jnp.bfloat16), "dp", scatter_dimension=0, tiled=True
        ).astype(jnp.float32),
    )
    shared = (
        lax.psum(shards[0].astype(jnp.bfloat16), "tensor").astype(jnp.float32),
        lax.psum(shards[2].astype(jnp.bfloat16), "tensor").astype(jnp.float32),
        lax.psum(shards[3].astype(jnp.bfloat16), "tensor").astype(jnp.float32),
        lax.psum(shards[4].astype(jnp.bfloat16), "tensor").astype(jnp.float32),
        lax.psum(shards[5].astype(jnp.bfloat16), "tensor").astype(jnp.float32),
        lax.psum(shards[7].astype(jnp.bfloat16), "tensor").astype(jnp.float32),
        lax.psum(shards[8].astype(jnp.bfloat16), "tensor").astype(jnp.float32),
        lax.psum(shards[12].astype(jnp.bfloat16), "tensor").astype(jnp.float32),
    )
    return (
        output,
        grad_hidden,
        shared[0],
        shards[1],
        shared[1],
        shared[2],
        shared[3],
        shared[4],
        shards[6],
        shared[5],
        shared[6],
        shards[9],
        shards[10],
        shards[11],
        shared[7],
    )


def solution(mesh):
    placed = (
        P(("dp", "tensor"), None),
        P("dp"),
        P("dp", "tensor"),
        P("dp", None),
        P("dp", None),
        P("dp"),
        P("dp"),
        P("tensor", "dp"),
        P("dp"),
        P("dp"),
        P("dp", "tensor"),
        P("dp", "tensor"),
        P("tensor", "dp"),
        P("dp"),
        P(("dp", "tensor"), None),
        P("dp"),
        P("dp"),
    )
    return jax.shard_map(
        local,
        mesh=mesh,
        in_specs=placed,
        out_specs=(
            P(("dp", "tensor"), None),
            P(("dp", "tensor"), None),
            P("dp"),
            P("dp", "tensor"),
            P("dp", None),
            P("dp", None),
            P("dp"),
            P("dp"),
            P("tensor", "dp"),
            P("dp"),
            P("dp"),
            P("dp", "tensor"),
            P("dp", "tensor"),
            P("tensor", "dp"),
            P("dp"),
        ),
        check_vma=False,
    )
```

profile of v0, /device:TPU:0, one launch (start us, length us, event | category | flops | bytes accessed | tf_op | source)
XLA Modules:
  0.0 1192.8 jit_solution(666818640022465522)
XLA Ops:
  15.8 39.0 %all-reduce.13 = (bf16[1152]{0:T(1024)(128)(2,1)S(1)}, bf16[1152]{0:T(1024)(128)(2,1)S(1)}, bf16[1152]{0:T(1024)(128)(2,1)S(1)}, bf16[256]{0:T(256)(128)(2,1)S(1...) all-reduce(bf16[1152]{0:T(1024)(128)(2,1)S(1)} %dynamic-update-slic, ...), channel_id=1, replica_groups=mesh['dp'=8,'tensor'=4] {'dp'}, use_global_device_ids=true, to_apply=%add.4 | all-reduce | flops 5120 | bytes 20480
  58.7 31.8 %all_gather.67 = bf16[1152,256]{1,0:T(8,128)(2,1)S(1)} all-gather(bf16[144,256]{1,0:T(8,128)(2,1)S(1)} %copy-done.33), channel_id=1, replica_groups=mesh['dp'=8,'tensor'=4] {'dp'}, dimensions={0}, use_global_device_ids=true | all-gather | bytes 663552 | tf_op jit(solution)/shard_map/all_gather | solution.py:95
  90.5 31.5 %all_gather.69 = bf16[1152,256]{1,0:T(8,128)(2,1)S(1)} all-gather(bf16[144,256]{1,0:T(8,128)(2,1)S(1)} %copy-done.34), channel_id=1, replica_groups=mesh['dp'=8,'tensor'=4] {'dp'}, dimensions={0}, use_global_device_ids=true | all-gather | bytes 663552 | tf_op jit(solution)/shard_map/all_gather | solution.py:94
  122.0 31.4 %all_gather.66 = bf16[1152,256]{1,0:T(8,128)(2,1)S(1)} all-gather(bf16[144,256]{1,0:T(8,128)(2,1)S(1)} %copy-done.35), channel_id=1, replica_groups=mesh['dp'=8,'tensor'=4] {'dp'}, dimensions={0}, use_global_device_ids=true | all-gather | bytes 663552 | tf_op jit(solution)/shard_map/all_gather | solution.py:96
  153.4 33.3 %all_gather.71 = bf16[256,1152]{0,1:T(8,128)(2,1)} all-gather(bf16[256,144]{0,1:T(8,128)(2,1)S(1)} %copy-done.36), channel_id=1, replica_groups=mesh['dp'=8,'tensor'=4] {'dp'}, dimensions={1}, use_global_device_ids=true | all-gather | bytes 663552 | tf_op jit(solution)/shard_map/all_gather | solution.py:99
  198.8 24.3 %reduce-scatter.12.cloned.1.call-done = bf16[160,1152]{1,0:T(8,128)(2,1)} async-done(((bf16[640,1152]{1,0:T(8,128)(2,1)}), bf16[160,1152]{1,0:T(8,128)(2,1)}) %reduce-scatter.12.cloned.1.call-update) | async-done | bytes 368656 | tf_op jit(solution)/shard_map/reduce_scatter | solution.py:138
  229.5 40.5 %all-gather.12.cloned.1.call-done = bf16[1152,1728]{1,0:T(8,128)(2,1)} async-done(((bf16[144,1728]{1,0:T(8,128)(2,1)}), bf16[1152,1728]{1,0:T(8,128)(2,1)}) %all-gather.12.cloned.1.call-update) | async-done | bytes 3981328 | tf_op jit(solution)/shard_map/all_gather | solution.py:144
  270.0 19.6 %all-gather.10.cloned.1.call-done = bf16[640,1152]{1,0:T(8,128)(2,1)} async-done(((bf16[160,1152]{1,0:T(8,128)(2,1)}), bf16[640,1152]{1,0:T(8,128)(2,1)}) %all-gather.10.cloned.1.call-update) | async-done | bytes 1474576 | tf_op jit(solution)/shard_map/all_gather | solution.py:151
  289.6 8.2 fusion.112
  297.8 65.6 %all-gather.14.cloned.1.call-done = bf16[1152,1728]{1,0:T(8,128)(2,1)} async-done(((bf16[144,1728]{1,0:T(8,128)(2,1)}), bf16[1152,1728]{1,0:T(8,128)(2,1)}) %all-gather.14.cloned.1.call-update) | async-done | bytes 3981328 | tf_op jit(solution)/shard_map/all_gather | solution.py:145
  363.4 11.3 multiply_convert_fusion.1
  374.7 61.3 %all-gather.16.cloned.1.call-done = bf16[1728,1152]{0,1:T(8,128)(2,1)} async-done(((bf16[1728,144]{0,1:T(8,128)(2,1)}), bf16[1728,1152]{0,1:T(8,128)(2,1)}) %all-gather.16.cloned.1.call-update) | async-done | bytes 3981328 | tf_op jit(solution)/shard_map/all_gather | solution.py:146
  436.0 7.2 convolution_convert_fusion.4
  443.3 26.1 %reduce-scatter.14.cloned.1.call-done = bf16[160,1152]{1,0:T(8,128)(2,1)} async-done(((bf16[640,1152]{1,0:T(8,128)(2,1)}), bf16[160,1152]{1,0:T(8,128)(2,1)}) %reduce-scatter.14.cloned.1.call-update) | async-done | bytes 368656 | tf_op jit(solution)/shard_map/reduce_scatter | solution.py:157
  474.8 19.0 %all-gather.18.cloned.1.call-done = bf16[640,1152]{1,0:T(8,128)(2,1)} async-done(((bf16[160,1152]{1,0:T(8,128)(2,1)}), bf16[640,1152]{1,0:T(8,128)(2,1)}) %all-gather.18.cloned.1.call-update) | async-done | bytes 1474576 | tf_op jit(solution)/shard_map/all_gather | solution.py:193
  493.9 10.5 multiply_convert_fusion
  508.1 4.5 fusion.8
  512.6 27.5 %reduce-scatter.16.cloned.1.call-done = bf16[160,1152]{1,0:T(8,128)(2,1)} async-done(((bf16[640,1152]{1,0:T(8,128)(2,1)}), bf16[160,1152]{1,0:T(8,128)(2,1)}) %reduce-scatter.16.cloned.1.call-update) | async-done | bytes 368656 | tf_op jit(solution)/shard_map/reduce_scatter | solution.py:201
  546.6 19.0 %all-gather.20.cloned.1.call-done = bf16[640,1152]{1,0:T(8,128)(2,1)} async-done(((bf16[160,1152]{1,0:T(8,128)(2,1)}), bf16[640,1152]{1,0:T(8,128)(2,1)}) %all-gather.20.cloned.1.call-update) | async-done | bytes 1474576 | tf_op jit(solution)/shard_map/all_gather | solution.py:207
  588.2 48.9 %reduce-scatter.24.cloned.1.call-done = bf16[144,256]{1,0:T(8,128)(2,1)} async-done(((bf16[1152,256]{1,0:T(8,128)(2,1)}), bf16[144,256]{1,0:T(8,128)(2,1)}) %reduce-scatter.24.cloned.1.call-update) | async-done | bytes 73744 | tf_op jit(solution)/shard_map/reduce_scatter | solution.py:263
  637.1 65.1 %reduce-scatter.22.cloned.1.call-done = bf16[144,256]{1,0:T(8,128)(2,1)} async-done(((bf16[1152,256]{1,0:T(8,128)(2,1)}), bf16[144,256]{1,0:T(8,128)(2,1)}) %reduce-scatter.22.cloned.1.call-update) | async-done | bytes 73744 | tf_op jit(solution)/shard_map/reduce_scatter | solution.py:260
  702.3 7.4 convolution_convert_fusion
  711.1 7.1 convolution_convert_fusion.2
  718.3 7.1 convolution_convert_fusion.1
  731.4 35.8 %reduce-scatter.26.cloned.1.call-done = bf16[256,144]{0,1:T(8,128)(2,1)} async-done(((bf16[256,1152]{0,1:T(8,128)(2,1)}), bf16[256,144]{0,1:T(8,128)(2,1)}) %reduce-scatter.26.cloned.1.call-update) | async-done | bytes 73744 | tf_op jit(solution)/shard_map/reduce_scatter | solution.py:278
  768.8 64.0 %reduce-scatter.20.cloned.1.call-done = bf16[144,256]{1,0:T(8,128)(2,1)} async-done(((bf16[1152,256]{1,0:T(8,128)(2,1)}), bf16[144,256]{1,0:T(8,128)(2,1)}) %reduce-scatter.20.cloned.1.call-update) | async-done | bytes 73744 | tf_op jit(solution)/shard_map/reduce_scatter | solution.py:257
  837.4 85.7 %reduce-scatter.32.cloned.1.call-done = bf16[1728,144]{0,1:T(8,128)(2,1)} async-done(((bf16[1728,1152]{0,1:T(8,128)(2,1)}), bf16[1728,144]{0,1:T(8,128)(2,1)}) %reduce-scatter.32.cloned.1.call-update) | async-done | bytes 497680 | tf_op jit(solution)/shard_map/reduce_scatter | solution.py:293
  925.2 89.0 %reduce-scatter.28.cloned.1.call-done = bf16[144,1728]{1,0:T(8,128)(2,1)} async-done(((bf16[1152,1728]{1,0:T(8,128)(2,1)}), bf16[144,1728]{1,0:T(8,128)(2,1)}) %reduce-scatter.28.cloned.1.call-update) | async-done | bytes 497680 | tf_op jit(solution)/shard_map/reduce_scatter | solution.py:287
  1016.2 88.8 %reduce-scatter.30.cloned.1.call-done = bf16[144,1728]{1,0:T(8,128)(2,1)} async-done(((bf16[1152,1728]{1,0:T(8,128)(2,1)}), bf16[144,1728]{1,0:T(8,128)(2,1)}) %reduce-scatter.30.cloned.1.call-update) | async-done | bytes 497680 | tf_op jit(solution)/shard_map/reduce_scatter | solution.py:290
  1107.1 27.5 %reduce-scatter.18.cloned.1.call-done = bf16[160,1152]{1,0:T(8,128)(2,1)} async-done(((bf16[640,1152]{1,0:T(8,128)(2,1)}), bf16[160,1152]{1,0:T(8,128)(2,1)}) %reduce-scatter.18.cloned.1.call-update) | async-done | bytes 368656 | tf_op jit(solution)/shard_map/reduce_scatter | solution.py:248
  1136.0 37.1 %all-reduce.12 = (bf16[1152]{0:T(1024)(128)(2,1)S(1)}, bf16[256]{0:T(256)(128)(2,1)S(1)}, bf16[256]{0:T(256)(128)(2,1)S(1)}, bf16[1152]{0:T(1024)(128)(2,1)S(1)}...) all-reduce(bf16[1152]{0:T(1024)(128)(2,1)S(1)} %get-tuple-element.2, ...), channel_id=6, replica_groups=mesh['dp'=8,'tensor'=4] {'dp'}, use_global_device_ids=true, to_apply=%region_19.20.clone | all-reduce | flops 5120 | bytes 20480
  1173.6 5.9 all-reduce.14
  (273 shorter events, 92.3 us)
Async XLA Ops:
  8.0 114.0 %copy-start.35 = (bf16[144,256]{1,0:T(8,128)(2,1)S(1)}, bf16[144,256]{1,0:T(8,128)(2,1)}, u32[]{:S(2)}) copy-start(bf16[144,256]{1,0:T(8,128)(2,1)} %param.21) | copy-start | bytes 221188
  8.0 178.7 %all-gather.8.cloned.1.call-start = ((), (), s32[]{:S(2)}) async-start(), calls=%async_computation.11 | async-start | bytes 1843200 | tf_op jit(solution)/shard_map/all_gather | solution.py:115
  56.0 130.8 %copy-start.45 = (f32[160]{0:T(256)}, f32[160]{0:T(256)S(1)}, u32[]{:S(2)}) copy-start(f32[160]{0:T(256)S(1)} %add_rsqrt_fusion.5) | copy-start | bytes 1924
  57.9 165.2 %reduce-scatter.12.cloned.1.call-start = ((), (), s32[]{:S(2)}) async-start(), calls=%async_computation.12 | async-start | bytes 1843200 | tf_op jit(solution)/shard_map/reduce_scatter | solution.py:138
  58.0 131.9 %copy-start.58 = (f32[256]{0:T(256)}, f32[256]{0:T(256)S(1)}, u32[]{:S(2)}) copy-start(f32[256]{0:T(256)S(1)} %convert_element_type.231) | copy-start | bytes 3076
  58.7 132.9 %copy-start.39 = (f32[640]{0:T(1024)}, f32[640]{0:T(1024)S(1)}, u32[]{:S(2)}) copy-start(f32[640]{0:T(1024)S(1)} %convert_element_type.232) | copy-start | bytes 7684
  58.7 132.8 %copy-start.56 = (f32[256]{0:T(256)}, f32[256]{0:T(256)S(1)}, u32[]{:S(2)}) copy-start(f32[256]{0:T(256)S(1)} %convert_element_type.233) | copy-start | bytes 3076
  58.7 132.9 %copy-start.60 = (f32[128]{0:T(128)}, f32[128]{0:T(128)S(1)}, u32[]{:S(2)}) copy-start(f32[128]{0:T(128)S(1)} %multiply_power_fusion) | copy-start | bytes 1540
  90.5 98.5 %copy-start.7 = (bf16[1152,256]{1,0:T(8,128)(2,1)}, bf16[1152,256]{1,0:T(8,128)(2,1)S(1)}, u32[]{:S(2)}) copy-start(bf16[1152,256]{1,0:T(8,128)(2,1)S(1)} %all_gather.67) | copy-start | bytes 1769476
  198.2 71.8 %all-gather.12.cloned.1.call-start = ((), (), s32[]{:S(2)}) async-start(), calls=%async_computation.14 | async-start | bytes 4644864 | tf_op jit(solution)/shard_map/all_gather | solution.py:144
  198.8 90.8 %all-gather.10.cloned.1.call-start = ((), (), s32[]{:S(2)}) async-start(), calls=%async_computation.13 | async-start | bytes 1843200 | tf_op jit(solution)/shard_map/all_gather | solution.py:151
  224.3 315.8 %copy-start.43 = (f32[160]{0:T(256)}, f32[160]{0:T(256)S(1)}, u32[]{:S(2)}) copy-start(f32[160]{0:T(256)S(1)} %add_rsqrt_fusion.4) | copy-start | bytes 1924
  225.6 314.5 %copy-start.52 = (f32[160]{0:T(256)}, f32[160]{0:T(256)S(1)}, u32[]{:S(2)}) copy-start(f32[160]{0:T(256)S(1)} %add_rsqrt_fusion.3) | copy-start | bytes 1924
  227.7 135.7 %all-gather.14.cloned.1.call-start = ((), (), s32[]{:S(2)}) async-start(), calls=%async_computation.15 | async-start | bytes 4644864 | tf_op jit(solution)/shard_map/all_gather | solution.py:145
  228.2 207.7 %all-gather.16.cloned.1.call-start = ((), (), s32[]{:S(2)}) async-start(), calls=%async_computation.16 | async-start | bytes 4644864 | tf_op jit(solution)/shard_map/all_gather | solution.py:146
  229.0 240.4 %reduce-scatter.14.cloned.1.call-start = ((), (), s32[]{:S(2)}) async-start(), calls=%async_computation.17 | async-start | bytes 1843200 | tf_op jit(solution)/shard_map/reduce_scatter | solution.py:157
  443.2 50.6 %all-gather.18.cloned.1.call-start = ((), (), s32[]{:S(2)}) async-start(), calls=%async_computation.18 | async-start | bytes 1843200 | tf_op jit(solution)/shard_map/all_gather | solution.py:193
  474.6 65.5 %reduce-scatter.16.cloned.1.call-start = ((), (), s32[]{:S(2)}) async-start(), calls=%async_computation.19 | async-start | bytes 1843200 | tf_op jit(solution)/shard_map/reduce_scatter | solution.py:201
  512.6 53.0 %all-gather.20.cloned.1.call-start = ((), (), s32[]{:S(2)}) async-start(), calls=%async_computation.20 | async-start | bytes 1843200 | tf_op jit(solution)/shard_map/all_gather | solution.py:207
  546.3 90.8 %reduce-scatter.24.cloned.1.call-start = ((), (), s32[]{:S(2)}) async-start(), calls=%async_computation.24 | async-start | bytes 663552 | tf_op jit(solution)/shard_map/reduce_scatter | solution.py:263
  574.3 128.0 %reduce-scatter.22.cloned.1.call-start = ((), (), s32[]{:S(2)}) async-start(), calls=%async_computation.23 | async-start | bytes 663552 | tf_op jit(solution)/shard_map/reduce_scatter | solution.py:260
  580.5 186.7 %reduce-scatter.26.cloned.1.call-start = ((), (), s32[]{:S(2)}) async-start(), calls=%async_computation.25 | async-start | bytes 663552 | tf_op jit(solution)/shard_map/reduce_scatter | solution.py:278
  583.2 249.6 %reduce-scatter.20.cloned.1.call-start = ((), (), s32[]{:S(2)}) async-start(), calls=%async_computation.22 | async-start | bytes 663552 | tf_op jit(solution)/shard_map/reduce_scatter | solution.py:257
  588.2 246.2 %all-reduce.18.cloned.1.call-start = ((), (), s32[]{:S(2)}) async-start(), calls=%async_computation.29 | async-start | bytes 294912 | tf_op jit(solution)/shard_map/psum | solution.py:302
  702.3 220.8 %reduce-scatter.32.cloned.1.call-start = ((), (), s32[]{:S(2)}) async-start(), calls=%async_computation.28 | async-start | bytes 4644864 | tf_op jit(solution)/shard_map/reduce_scatter | solution.py:293
  709.8 304.4 %reduce-scatter.28.cloned.1.call-start = ((), (), s32[]{:S(2)}) async-start(), calls=%async_computation.26 | async-start | bytes 4644864 | tf_op jit(solution)/shard_map/reduce_scatter | solution.py:287
  718.2 386.8 %reduce-scatter.30.cloned.1.call-start = ((), (), s32[]{:S(2)}) async-start(), calls=%async_computation.27 | async-start | bytes 4644864 | tf_op jit(solution)/shard_map/reduce_scatter | solution.py:290
  725.4 409.2 %reduce-scatter.18.cloned.1.call-start = ((), (), s32[]{:S(2)}) async-start(), calls=%async_computation.21 | async-start | bytes 1843200 | tf_op jit(solution)/shard_map/reduce_scatter | solution.py:248
  925.2 209.4 %copy-start.46 = (f32[160]{0:T(256)S(1)}, f32[160]{0:T(256)}, u32[]{:S(2)}) copy-start(f32[160]{0:T(256)} %copy-done.45) | copy-start | bytes 1924
  925.2 210.8 %copy-start.49 = (bf16[1152]{0:T(1024)(128)(2,1)S(1)}, bf16[1152]{0:T(1024)(128)(2,1)}, u32[]{:S(2)}) copy-start(bf16[1152]{0:T(1024)(128)(2,1)} %get-tuple-element.23) | copy-start | bytes 6916
  925.2 210.8 %copy-start.50 = (bf16[1152]{0:T(1024)(128)(2,1)S(1)}, bf16[1152]{0:T(1024)(128)(2,1)}, u32[]{:S(2)}) copy-start(bf16[1152]{0:T(1024)(128)(2,1)} %get-tuple-element.19) | copy-start | bytes 6916
  925.2 210.8 %copy-start.51 = (bf16[1152]{0:T(1024)(128)(2,1)S(1)}, bf16[1152]{0:T(1024)(128)(2,1)}, u32[]{:S(2)}) copy-start(bf16[1152]{0:T(1024)(128)(2,1)} %get-tuple-element.21) | copy-start | bytes 6916
  (56 other events, 615.3 us)
Sparse Core Ops, SparseCore 0:
  58.0 16.3 all-gather.7
  198.3 24.7 reduce-scatter.11
  443.4 26.0 reduce-scatter.13
  474.7 19.0 all-gather.17
  512.7 27.3 reduce-scatter.15
  546.5 19.0 all-gather.19
  702.4 30.1 all-reduce.17
Sparse Core Ops, SparseCore 1:
  200.9 69.1 all-gather.11
  272.0 17.5 all-gather.9
  291.7 71.7 all-gather.13
  365.6 70.3 all-gather.15
  574.4 62.7 reduce-scatter.23
  640.5 61.7 reduce-scatter.21
  705.4 61.7 reduce-scatter.25
  770.9 61.7 reduce-scatter.19
  836.2 86.9 reduce-scatter.31
  926.7 87.4 reduce-scatter.27
  1017.6 87.4 reduce-scatter.29
  1107.7 26.9 reduce-scatter.17
where the time goes:
time: 1200 us; the launch traced here: 1190 us
  waiting for transfers between devices  810 us (68%)
  blocking collectives  210 us (18%)
  matrix products  88.4 us (7%)
  other arithmetic  48.7 us (4%)
  between operations  19.6 us (2%)
  local copies, waits for them, and re-layouts  14.6 us (1%)
    reduce_scatter x1, waiting for transfers between devices, local(): lax.psum_scatter(grad_wg.astype(jnp.bfloat16), 'dp', scatter_dimension=0,...  89 us
    reduce_scatter x1, waiting for transfers between devices, local(): lax.psum_scatter(grad_wu.astype(jnp.bfloat16), 'dp', scatter_dimension=0,...  88.8 us
    reduce_scatter x1, waiting for transfers between devices, local(): lax.psum_scatter(grad_wd.astype(jnp.bfloat16), 'dp', scatter_dimension=1,...  85.7 us
    unnamed x2, blocking collectives  76.1 us
    all_gather x1, waiting for transfers between devices, local(): lax.all_gather(w_up, 'dp', axis=0, tiled=True)  65.6 us
    reduce_scatter x1, waiting for transfers between devices, local(): lax.psum_scatter(grad_wk.astype(jnp.bfloat16), 'dp', scatter_dimension=0,...  65.1 us
    reduce_scatter x1, waiting for transfers between devices, local(): lax.psum_scatter(grad_wq.astype(jnp.bfloat16), 'dp', scatter_dimension=0,...  64 us
    all_gather x1, waiting for transfers between devices, local(): lax.all_gather(w_down, 'dp', axis=1, tiled=True)  61.3 us
  transfers between devices with their start and end apart: 19, of which 17 were waited for; matrix products, arithmetic and copies ran while one was open for 6% of the time, Pallas kernels for 0%

commit v1 on v0

v1 whole, which is shorter than its diff:
```python
import functools

import jax
import jax.numpy as jnp
from jax import lax
from jax.experimental import pallas as pl
from jax.experimental.pallas import tpu as pltpu
from jax.sharding import PartitionSpec as P

HD = 256
WINDOW = 512


EPSILON = 1e-06
ROPE_BASE = 10000.0


def rms_scale(values):
    return lax.rsqrt(jnp.mean(values * values, axis=-1, keepdims=True) + EPSILON)


def apply_norm(values, gain_vec):
    return values * rms_scale(values) * gain_vec.astype(jnp.float32)


def norm_back(values, gain_vec, upstream):
    factor = rms_scale(values)
    unit_rows = values * factor
    scaled = upstream * gain_vec.astype(jnp.float32)
    grad_values = factor * (
        scaled - unit_rows * jnp.mean(scaled * unit_rows, axis=-1, keepdims=True)
    )
    return (grad_values, upstream * unit_rows)


def rotary_tables(token_pos, width):
    steps_half = jnp.arange(width // 2, dtype=jnp.float32)
    frequency = ROPE_BASE ** (-2.0 * steps_half / width)
    angles = token_pos.astype(jnp.float32)[:, None] * frequency[None, :]
    return (jnp.cos(angles), jnp.sin(angles))


def rotate(values, cosine, sine_table):
    half_width = values.shape[-1] // 2
    first_half = values[..., :half_width]
    second = values[..., half_width:]
    return jnp.concatenate(
        [first_half * cosine - second * sine_table, second * cosine + first_half * sine_table],
        axis=-1,
    )


def window_mask(seq_ids):
    length_seq = seq_ids.shape[0]
    token_index = jnp.arange(length_seq, dtype=jnp.int32)
    behind = token_index[:, None] - token_index[None, :]
    return (seq_ids[:, None] == seq_ids[None, :]) & (behind >= 0) & (behind < WINDOW)


def gelu_tanh(values):
    return jax.nn.gelu(values, approximate=True)


def contract_rows(left, right):
    return lax.dot_general(
        left, right, (((0,), (0,)), ((), ())), preferred_element_type=jnp.float32
    )


def contract_cols(left, right):
    return lax.dot_general(
        left, right, (((1,), (1,)), ((), ())), preferred_element_type=jnp.float32
    )


MESH = pl.DeviceIdType.MESH
LANES = 128
SUBLANES = 16


def pieces_of(shapes, wanted):
    pieces = []
    for index, (rows, _) in enumerate(shapes):
        cuts = wanted if rows % (wanted * SUBLANES) == 0 else 1
        size = rows // cuts
        pieces.extend((index, cut * size, size) for cut in range(cuts))
    return pieces


def place_of(axis, n):
    me = lax.axis_index(axis)
    line = me // 2
    side = me - 2 * line
    return me, line, side, 2 * line + 1 - side, n // 2


def greet(partners):
    barrier = pltpu.get_barrier_semaphore()
    for name, index in partners:
        pl.semaphore_signal(barrier, inc=1, device_id={name: index}, device_id_type=MESH)
    pl.semaphore_wait(barrier, len(partners))


def remote(axis, target, src, dst, send, recv):
    return pltpu.make_async_remote_copy(
        src_ref=src,
        dst_ref=dst,
        send_sem=send,
        recv_sem=recv,
        device_id={axis: target},
        device_id_type=MESH,
    )


def gather_body(axis, n, pieces, count, *refs):
    ins, outs = refs[:count], refs[count : 2 * count]
    own_sem, far_send, far_recv, near_send, near_recv = refs[2 * count :]
    me, line, side, mate, length = place_of(axis, n)
    ahead = [2 * ((line + k) % length) + side for k in range(length)]
    behind = [2 * ((line + length - k) % length) + side for k in range(length)]
    greet([(axis, ahead[k]) for k in range(1, length)] + [(axis, mate)])

    def far(c, k):
        a, row, size = pieces[c]
        rows = pl.ds(row, size)
        return remote(
            axis, ahead[k], ins[a].at[rows], outs[a].at[me, rows],
            far_send.at[c, k], far_recv.at[c, k],
        )

    def near(c, k):
        a, row, size = pieces[c]
        rows = pl.ds(row, size)
        source = ins[a].at[rows] if k == 0 else outs[a].at[behind[k], rows]
        return remote(
            axis, mate, source, outs[a].at[behind[k], rows],
            near_send.at[c, k], near_recv.at[c, k],
        )

    for c in range(len(pieces)):
        for k in range(1, length):
            far(c, k).start()
        near(c, 0).start()
    own = [
        pltpu.make_async_copy(ins[a], outs[a].at[me], own_sem.at[a]) for a in range(count)
    ]
    for copy in own:
        copy.start()
    for c in range(len(pieces)):
        for k in range(1, length):
            far(c, k).wait_recv()
            near(c, k).start()
    for copy in own:
        copy.wait()
    for c in range(len(pieces)):
        for k in range(length):
            if k:
                far(c, k).wait_send()
            near(c, k).wait()


def gather(axis, n, arrays, wanted, ident):
    shapes = [array.shape for array in arrays]
    pieces = pieces_of(shapes, wanted)
    count = len(arrays)
    sems = pltpu.SemaphoreType.DMA((len(pieces), n // 2))
    return pl.pallas_call(
        functools.partial(gather_body, axis, n, pieces, count),
        out_shape=[jax.ShapeDtypeStruct((n, *array.shape), array.dtype) for array in arrays],
        in_specs=[pl.BlockSpec(memory_space=pltpu.VMEM)] * count,
        out_specs=[pl.BlockSpec(memory_space=pl.ANY)] * count,
        scratch_shapes=[pltpu.SemaphoreType.DMA((count,)), sems, sems, sems, sems],
        compiler_params=pltpu.CompilerParams(collective_id=ident, has_side_effects=True),
        name=f"gather{ident}",
    )(*arrays)


def by_rows(row, size, body):
    step = SUBLANES if size % SUBLANES == 0 else size
    if step == size:
        body(pl.ds(row, size))
        return

    def one(i, carry):
        body(pl.ds(pl.multiple_of(row + i * step, step), step))
        return carry

    lax.fori_loop(0, size // step, one, 0)


def scatter_body(axis, n, pieces, count, shared, other, n_other, *refs):
    ins, outs = refs[:count], refs[count : 2 * count]
    held, come = refs[2 * count : 3 * count], refs[3 * count : 4 * count]
    pools = refs[4 * count : 4 * count + len(shared)]
    sems = refs[4 * count + len(shared) :]
    far_send, far_recv, near_send, near_recv = sems[:4]
    me, line, side, mate, length = place_of(axis, n)
    ahead = [2 * ((line + k) % length) + side for k in range(length)]
    ahead_mate = [2 * ((line + k) % length) + 1 - side for k in range(length)]
    partners = [(axis, ahead[k]) for k in range(1, length)] + [(axis, mate)]
    if shared:
        spot = lax.axis_index(other)
        fellows = [(spot + j) % n_other for j in range(n_other)]
        partners += [(other, fellows[j]) for j in range(1, n_other)]
    greet(partners)
    order = list(range(1, length)) + [0]

    def near(c, k):
        a, row, size = pieces[c]
        rows = pl.ds(row, size)
        return remote(
            axis, mate, ins[a].at[ahead_mate[k], rows], held[a].at[k, rows],
            near_send.at[c, k], near_recv.at[c, k],
        )

    def far(c, k):
        a, row, size = pieces[c]
        rows = pl.ds(row, size)
        return remote(
            axis, ahead[k], held[a].at[k, rows], come[a].at[k - 1, rows],
            far_send.at[c, k], far_recv.at[c, k],
        )

    for c in range(len(pieces)):
        for k in order:
            near(c, k).start()
    waiting = None
    for c, (a, row, size) in enumerate(pieces):
        for k in order:
            near(c, k).wait_recv()

            def pair(rows, a=a, k=k):
                total = ins[a][ahead[k], rows].astype(jnp.float32) + held[a][k, rows].astype(
                    jnp.float32
                )
                if k == 0:
                    outs[a][rows] = total
                else:
                    held[a][k, rows] = total.astype(jnp.bfloat16)

            by_rows(row, size, pair)
            if waiting is not None:
                far(*waiting).start()
            waiting = (c, k) if k else None
    if waiting is not None:
        far(*waiting).start()
    for c, (a, row, size) in enumerate(pieces):
        for k in range(1, length):
            far(c, k).wait_recv()

        def add(rows, a=a):
            total = outs[a][rows]
            for k in range(1, length):
                total = total + come[a][k - 1, rows].astype(jnp.float32)
            outs[a][rows] = total

        by_rows(row, size, add)
    if shared:
        share_send, share_recv = sems[4:]

        def share(i, j):
            return remote(
                other, fellows[j], pools[i].at[spot], pools[i].at[spot],
                share_send.at[i, j], share_recv.at[i, j],
            )

        for i, a in enumerate(shared):
            pools[i][spot] = outs[a][...].astype(jnp.bfloat16)
        for i in range(len(shared)):
            for j in range(1, n_other):
                share(i, j).start()
        for i, a in enumerate(shared):
            for j in range(1, n_other):
                share(i, j).wait()
            total = pools[i][0].astype(jnp.float32)
            for j in range(1, n_other):
                total = total + pools[i][j].astype(jnp.float32)
            outs[a][...] = total
    for c in range(len(pieces)):
        for k in range(length):
            near(c, k).wait_send()
            if k:
                far(c, k).wait_send()


def scatter(axis, n, arrays, wanted, ident, shared=(), other=None, n_other=1):
    shapes = [array.shape[1:] for array in arrays]
    pieces = pieces_of(shapes, wanted)
    count = len(arrays)
    length = n // 2
    sems = pltpu.SemaphoreType.DMA((len(pieces), length))
    share_sems = [pltpu.SemaphoreType.DMA((len(shared), n_other))] * 2 if shared else []
    return pl.pallas_call(
        functools.partial(scatter_body, axis, n, pieces, count, shared, other, n_other),
        out_shape=[jax.ShapeDtypeStruct(shape, jnp.float32) for shape in shapes],
        in_specs=[pl.BlockSpec(memory_space=pltpu.VMEM)] * count,
        out_specs=[pl.BlockSpec(memory_space=pltpu.VMEM)] * count,
        scratch_shapes=[pltpu.VMEM((length, *shape), jnp.bfloat16) for shape in shapes]
        + [pltpu.VMEM((length - 1, *shape), jnp.bfloat16) for shape in shapes]
        + [pltpu.VMEM((n_other, *shapes[a]), jnp.bfloat16) for a in shared]
        + [sems, sems, sems, sems]
        + share_sems,
        compiler_params=pltpu.CompilerParams(
            collective_id=ident, has_side_effects=True, vmem_limit_bytes=60 * 1024 * 1024
        ),
        name=f"scatter{ident}",
    )(*arrays)


def pack_gains(blocks, width):
    n = blocks[0].shape[0]
    rows = [jnp.pad(block, ((0, 0), (0, width - block.shape[1]))) for block in blocks]
    packed = jnp.stack(rows, axis=1)
    return jnp.pad(packed, ((0, 0), (0, SUBLANES - len(blocks)), (0, 0)))


def local(
    n_dp,
    n_tensor,
    hidden,
    in_gain,
    w_query,
    w_key,
    w_value,
    query_gain,
    key_gain,
    w_output,
    attn_gain,
    ffn_gain,
    w_gate,
    w_up,
    w_down,
    out_gain,
    cotangent,
    segment_ids,
    positions,
):
    factor = HD ** (-0.5)
    gains = (in_gain, attn_gain, ffn_gain, out_gain, query_gain, key_gain)
    width = -(-max(gain.shape[0] for gain in gains) // LANES) * LANES
    gain_rows = pack_gains([gain[None] for gain in gains], width)[0]
    attn_full = gather(
        "dp", n_dp, [gain_rows, w_query, w_key, w_value, w_output.T], 1, 0
    )
    full_in_gain, full_attn_gain, full_ffn_gain, full_out_gain, full_qgain, full_kgain = (
        attn_full[0][:, row, : gain.shape[0]].reshape(-1) for row, gain in enumerate(gains)
    )
    full_query, full_key, full_value, full_output = (
        block.reshape(-1, block.shape[-1]) for block in attn_full[1:]
    )
    heads_local = full_query.shape[1] // HD
    hidden_f = hidden.astype(jnp.float32)
    normed_local = apply_norm(hidden_f, full_in_gain).astype(jnp.bfloat16)
    normed_in = gather("tensor", n_tensor, [normed_local], 2, 2)[0].reshape(-1, normed_local.shape[-1])
    seq_len = normed_in.shape[0]
    query_raw = jnp.dot(normed_in, full_query, preferred_element_type=jnp.float32).reshape(
        seq_len, heads_local, HD
    )
    key_raw = jnp.dot(normed_in, full_key, preferred_element_type=jnp.float32)
    value_rows = jnp.dot(normed_in, full_value, preferred_element_type=jnp.float32).astype(
        jnp.bfloat16
    )
    cosine, sine_table = rotary_tables(positions, HD)
    query_rot = rotate(
        apply_norm(query_raw, full_qgain), cosine[:, None, :], sine_table[:, None, :]
    ).astype(jnp.bfloat16)
    key_rot = rotate(apply_norm(key_raw, full_kgain), cosine, sine_table).astype(jnp.bfloat16)
    allowed = window_mask(segment_ids)[None]
    scores = (
        jnp.einsum("qhd,kd->hqk", query_rot, key_rot, preferred_element_type=jnp.float32) * factor
    )
    log_total = jnp.log(jnp.sum(jnp.where(allowed, jnp.exp(scores), 0.0), axis=-1, keepdims=True))
    probs_low = jnp.where(allowed, jnp.exp(scores - log_total), 0.0).astype(jnp.bfloat16)
    context = jnp.einsum("hqk,kd->qhd", probs_low, value_rows, preferred_element_type=jnp.float32)
    context = context.reshape(seq_len, heads_local * HD).astype(jnp.bfloat16)
    attn_part = contract_cols(context, full_output)
    attn_rows = scatter(
        "tensor",
        n_tensor,
        [attn_part.astype(jnp.bfloat16).reshape(n_tensor, -1, attn_part.shape[-1])],
        2,
        6,
    )[0]
    residual = hidden_f + apply_norm(attn_rows, full_attn_gain)
    full_gate, full_up, full_down = (
        block.reshape(-1, block.shape[-1])
        for block in gather("dp", n_dp, [w_gate, w_up, w_down.T], 3, 1)
    )
    ffn_local = apply_norm(residual, full_ffn_gain).astype(jnp.bfloat16)
    ffn_in = gather("tensor", n_tensor, [ffn_local], 2, 3)[0].reshape(-1, ffn_local.shape[-1])
    gate_pre = jnp.dot(ffn_in, full_gate, preferred_element_type=jnp.float32)
    up_pre = jnp.dot(ffn_in, full_up, preferred_element_type=jnp.float32)
    gelu_values, gelu_back = jax.vjp(gelu_tanh, gate_pre)
    mixed = (gelu_values * up_pre).astype(jnp.bfloat16)
    down_part = contract_cols(mixed, full_down)
    down_rows = scatter(
        "tensor",
        n_tensor,
        [down_part.astype(jnp.bfloat16).reshape(n_tensor, -1, down_part.shape[-1])],
        2,
        7,
    )[0]
    output = (residual + apply_norm(down_rows, full_out_gain)).astype(jnp.bfloat16)
    cot_f = cotangent.astype(jnp.float32)
    grad_down, term_out = norm_back(down_rows, full_out_gain, cot_f)
    down_all = gather("tensor", n_tensor, [grad_down.astype(jnp.bfloat16)], 2, 4)[0].reshape(-1, grad_down.shape[-1])
    grad_wd = contract_rows(down_all, mixed)
    grad_mixed = jnp.dot(down_all, full_down, preferred_element_type=jnp.float32)
    gate_low = gelu_back(grad_mixed * up_pre)[0].astype(jnp.bfloat16)
    up_low = (grad_mixed * gelu_values).astype(jnp.bfloat16)
    grad_wg = contract_rows(ffn_in, gate_low)
    grad_wu = contract_rows(ffn_in, up_low)
    ffn_part = contract_cols(gate_low, full_gate) + contract_cols(up_low, full_up)
    ffn_back = scatter(
        "tensor",
        n_tensor,
        [ffn_part.astype(jnp.bfloat16).reshape(n_tensor, -1, ffn_part.shape[-1])],
        2,
        8,
    )[0]
    resid_norm, term_ffn = norm_back(residual, full_ffn_gain, ffn_back)
    grad_residual = cot_f + resid_norm
    grad_attn, term_attn = norm_back(attn_rows, full_attn_gain, grad_residual)
    attn_all = gather("tensor", n_tensor, [grad_attn.astype(jnp.bfloat16)], 2, 5)[0].reshape(-1, grad_attn.shape[-1])
    grad_wo = contract_rows(attn_all, context)
    grad_context = (
        jnp.dot(attn_all, full_output, preferred_element_type=jnp.float32)
        .astype(jnp.bfloat16)
        .reshape(seq_len, heads_local, HD)
    )
    scores_again = (
        jnp.einsum("qhd,kd->hqk", query_rot, key_rot, preferred_element_type=jnp.float32) * factor
    )
    probs = jnp.where(allowed, jnp.exp(scores_again - log_total), 0.0)
    grad_probs = jnp.einsum(
        "qhd,kd->hqk", grad_context, value_rows, preferred_element_type=jnp.float32
    )
    delta = jnp.sum(probs * grad_probs, axis=-1, keepdims=True)
    grad_scores = (probs * (grad_probs - delta) * factor).astype(jnp.bfloat16)
    value_heads = jnp.einsum(
        "hqk,qhd->khd", probs.astype(jnp.bfloat16), grad_context, preferred_element_type=jnp.float32
    ).astype(jnp.bfloat16)
    grad_qrot = jnp.einsum("hqk,kd->qhd", grad_scores, key_rot, preferred_element_type=jnp.float32)
    grad_kheads = jnp.einsum(
        "hqk,qhd->khd", grad_scores, query_rot, preferred_element_type=jnp.float32
    )
    grad_qraw, term_qgain = norm_back(
        query_raw, full_qgain, rotate(grad_qrot, cosine[:, None, :], -sine_table[:, None, :])
    )
    grad_kraw, term_kgain = norm_back(
        key_raw[:, None, :],
        full_kgain,
        rotate(grad_kheads, cosine[:, None, :], -sine_table[:, None, :]),
    )
    query_low = grad_qraw.astype(jnp.bfloat16).reshape(seq_len, heads_local * HD)
    key_low = grad_kraw.astype(jnp.bfloat16)
    grad_wq = contract_rows(normed_in, query_low)
    grad_wk = jnp.einsum("sd,she->de", normed_in, key_low, preferred_element_type=jnp.float32)
    grad_wv = jnp.einsum("sd,she->de", normed_in, value_heads, preferred_element_type=jnp.float32)
    attn_in_part = contract_cols(query_low, full_query)
    attn_in_part = attn_in_part + jnp.einsum(
        "she,de->sd", key_low, full_key, preferred_element_type=jnp.float32
    )
    attn_in_part = attn_in_part + jnp.einsum(
        "she,de->sd", value_heads, full_value, preferred_element_type=jnp.float32
    )
    attn_back = scatter(
        "tensor",
        n_tensor,
        [attn_in_part.astype(jnp.bfloat16).reshape(n_tensor, -1, attn_in_part.shape[-1])],
        2,
        9,
    )[0]
    in_norm, term_in = norm_back(hidden_f, full_in_gain, attn_back)
    grad_hidden = grad_residual + in_norm
    def blocks(values):
        return values.astype(jnp.bfloat16).reshape(n_dp, -1, values.shape[-1])

    ffn_grads = scatter(
        "dp", n_dp, [blocks(grad_wg), blocks(grad_wu), blocks(grad_wd)], 3, 10
    )
    gain_grads = [
        jnp.sum(term, axis=tuple(range(term.ndim - 1))).astype(jnp.bfloat16).reshape(n_dp, -1)
        for term in (term_in, term_attn, term_ffn, term_out, term_qgain, term_kgain)
    ]
    attn_grads = scatter(
        "dp",
        n_dp,
        [
            blocks(grad_wk),
            blocks(grad_wv),
            pack_gains(gain_grads, width),
            blocks(grad_wq),
            blocks(grad_wo),
        ],
        1,
        11,
        shared=(0, 1, 2),
        other="tensor",
        n_other=n_tensor,
    )
    own_in, own_attn, own_ffn, own_out, own_q, own_k = (
        attn_grads[2][row, : gain.shape[0]] for row, gain in enumerate(gains)
    )
    return (
        output,
        grad_hidden,
        own_in,
        attn_grads[3],
        attn_grads[0],
        attn_grads[1],
        own_q,
        own_k,
        attn_grads[4].T,
        own_attn,
        own_ffn,
        ffn_grads[0],
        ffn_grads[1],
        ffn_grads[2].T,
        own_out,
    )


def solution(mesh):
    placed = (
        P(("dp", "tensor"), None),
        P("dp"),
        P("dp", "tensor"),
        P("dp", None),
        P("dp", None),
        P("dp"),
        P("dp"),
        P("tensor", "dp"),
        P("dp"),
        P("dp"),
        P("dp", "tensor"),
        P("dp", "tensor"),
        P("tensor", "dp"),
        P("dp"),
        P(("dp", "tensor"), None),
        P("dp"),
        P("dp"),
    )
    return jax.shard_map(
        functools.partial(local, mesh.shape["dp"], mesh.shape["tensor"]),
        mesh=mesh,
        in_specs=placed,
        out_specs=(
            P(("dp", "tensor"), None),
            P(("dp", "tensor"), None),
            P("dp"),
            P("dp", "tensor"),
            P("dp", None),
            P("dp", None),
            P("dp"),
            P("dp"),
            P("tensor", "dp"),
            P("dp"),
            P("dp"),
            P("dp", "tensor"),
            P("dp", "tensor"),
            P("tensor", "dp"),
            P("dp"),
        ),
        check_vma=False,
    )
```

time: 1200 us -> 673 us (0.56)
  waiting for transfers between devices: 810 us -> 0 us
  Pallas kernels: 0 us -> 516 us
  blocking collectives: 210 us -> 0 us
  local copies, waits for them, and re-layouts: 14.6 us -> 41.3 us
  other arithmetic: 48.7 us -> 29.4 us
  between operations: 19.6 us -> 2 us
    reduce_scatter x11 -> x0, waiting for transfers between devices: 583 us -> none  [the longest x1 89 us: local(): lax.psum_scatter(grad_wg.astype(jnp.bfloat16), 'dp', scatter_dimension=0,...]
    pallas_call x0 -> x12, Pallas kernels: none -> 516 us  [the longest x6 262 us: scatter(): pl.pallas_call(functools.partial(scatter_body, axis, n, pieces, count, sh...]
    all_gather x7 -> x0, waiting for transfers between devices: 225 us -> none  [the longest x1 65.6 us: local(): lax.all_gather(w_up, 'dp', axis=0, tiled=True)]
    all_gather x4 -> x0, blocking collectives: 128 us -> none  [the longest x1 33.3 us: local(): lax.all_gather(w_output, 'dp', axis=1, tiled=True)]
    unnamed x2 -> x0, blocking collectives: 76.1 us -> none
    convert_element_type x0 -> x15, local copies, waits for them, and re-layouts: none -> 21.2 us  [the longest x3 19.4 us: blocks(): return values.astype(jnp.bfloat16).reshape(n_dp, -1, values.shape[-1])]
    convert_element_type x13 -> x0, other arithmetic: 15.7 us -> none  [the longest x5 9.31 us: local(): shards = (lax.psum_scatter(jnp.sum(term_in, axis=0).astype(jnp.bfloat16),...]
  transfers between devices with their start and end apart: 19 -> 0, of which waited for: 17 -> 0; matrix products, arithmetic and copies ran while one was open for 6% -> 0% of each run, Pallas kernels for 0% -> 0%
where the time goes in v1:
time: 673 us; the launch traced here: 667 us
  Pallas kernels  516 us (77%)
  matrix products  78 us (12%)
  local copies, waits for them, and re-layouts  41.3 us (6%)
  other arithmetic  29.4 us (4%)
    pallas_call x6, Pallas kernels, scatter(): pl.pallas_call(functools.partial(scatter_body, axis, n, pieces, count, sh...  262 us
    pallas_call x6, Pallas kernels, gather(): pl.pallas_call(functools.partial(gather_body, axis, n, pieces, count), ou...  254 us
    dot_general x5, matrix products, contract_rows(): lax.dot_general(left, right, (((0,), (0,)), ((), ())), preferred_element_...  24 us
    convert_element_type x3, local copies, waits for them, and re-layouts, blocks(): return values.astype(jnp.bfloat16).reshape(n_dp, -1, values.shape[-1])  19.4 us
    dot_general x5, matrix products, contract_cols(): lax.dot_general(left, right, (((1,), (1,)), ((), ())), preferred_element_...  14.5 us

profile of v1, /device:TPU:0, one launch (start us, length us, event | category | flops | bytes accessed | tf_op | source)
XLA Modules:
  0.0 666.6 jit_solution(9960174984590834872)
XLA Ops:
  4.6 40.2 %gather0.1 = (bf16[8,16,256]{2,1,0:T(8,128)(2,1)}, bf16[8,144,256]{2,1,0:T(8,128)(2,1)}, bf16[8,144,256]{2,1,0:T(8,128)(2,1)}, bf16[8,144,256]{2,1,0:T(8,128)(2,1)}, bf16[8,144,256]{2,1,0:T(8,128)(2,1)}) custom-call(bf16[16,256]{1,0:T(8,128)(2,1)} %pad_bitcast_fusion.refs_0_, bf16[144,256]{1,0:T(8,128)(2,1)} %refs_1_.2, bf16[144,256]{1,0:T(8,128)(2,1)} %refs_2_.1, ...), custom_call_target="tpu_custom_call" | custom-call | tf_op jit(solution)/shard_map/gather0/pallas_call | solution.py:167
  47.8 1.9 fusion.34.refs_0_
  49.7 13.4 %gather2.1 = bf16[4,160,1152]{2,1,0:T(8,128)(2,1)} custom-call(bf16[160,1152]{1,0:T(8,128)(2,1)} %fusion.34.refs_0_), custom_call_target="tpu_custom_call" | custom-call | tf_op jit(solution)/shard_map/gather2/pallas_call | solution.py:167
  63.1 2.9 convolution_convert_fusion.12
  68.9 2.1 fusion.77
  74.0 2.1 fusion.60
  80.3 15.5 %scatter6.1 = f32[160,1152]{1,0:T(8,128)} custom-call(bf16[4,160,1152]{2,1,0:T(8,128)(2,1)} %bitcast.215), custom_call_target="tpu_custom_call" | custom-call | tf_op jit(solution)/shard_map/scatter6/pallas_call | solution.py:293
  99.4 13.0 %gather3.1 = bf16[4,160,1152]{2,1,0:T(8,128)(2,1)} custom-call(bf16[160,1152]{1,0:T(8,128)(2,1)} %multiply_convert_fusion.3.refs_0_), custom_call_target="tpu_custom_call" | custom-call | tf_op jit(solution)/shard_map/gather3/pallas_call | solution.py:167
  112.4 161.2 %gather1.1 = (bf16[8,144,1728]{2,1,0:T(8,128)(2,1)}, bf16[8,144,1728]{2,1,0:T(8,128)(2,1)}, bf16[8,144,1728]{2,1,0:T(8,128)(2,1)}) custom-call(bf16[144,1728]{1,0:T(8,128)(2,1)} %refs_0_.1, bf16[144,1728]{1,0:T(8,128)(2,1)} %refs_1_.3, bf16[144,1728]{1,0:T(8,128)(2,1)} %bitcast.239), custom_call_target="tpu_custom_call" | custom-call | tf_op jit(solution)/shard_map/gather1/pallas_call | solution.py:167
  273.7 6.5 fusion.92
  280.2 6.7 %multiply_convert_fusion.1 = (bf16[640,1728]{0,1:T(8,128)(2,1)S(1)}, f32[640,1728]{0,1:T(8,128)}) fusion(f32[640,1728]{0,1:T(8,128)S(1)} %fusion.92, bf16[640,1152]{1,0:T(8,128)(2,1)S(1)} %bitcast.221, bf16[1152,1728]{1,0:T(8,128)(2,1)S(1)} %bitcast.248), kind=kOutput, calls=%fused_computation.13 | convolution fusion | flops 2559098880 | bytes 16515072 | tf_op jit(solution)/shard_map/dot_general | solution.py:392
  286.9 4.5 convolution_convert_fusion.4
  291.4 14.2 %scatter7.1 = f32[160,1152]{1,0:T(8,128)} custom-call(bf16[4,160,1152]{2,1,0:T(8,128)(2,1)} %bitcast.229), custom_call_target="tpu_custom_call" | custom-call | tf_op jit(solution)/shard_map/scatter7/pallas_call | solution.py:293
  308.7 2.1 fusion.33
  310.8 13.4 %gather4.1 = bf16[4,160,1152]{2,1,0:T(8,128)(2,1)} custom-call(bf16[160,1152]{1,0:T(8,128)(2,1)} %get-tuple-element.70.refs_0_), custom_call_target="tpu_custom_call" | custom-call | tf_op jit(solution)/shard_map/gather4/pallas_call | solution.py:167
  324.2 10.5 %multiply_convert_fusion = (bf16[640,1728]{0,1:T(8,128)(2,1)S(1)}, bf16[640,1728]{0,1:T(8,128)(2,1)S(1)}) fusion(f32[640,1728]{0,1:T(8,128)} %copy-done.60, f32[640,1728]{0,1:T(8,128)} %get-tuple-element.95, bf16[640,1152]{1,0:T(8,128)(2,1)} %bitcast.224, bf16[1152,1728]{1,0:T(8,128)(2,1)} %bitcast.252), kind=kOutput, calls=%fused_computation.12 | convolution fusion | flops 2574581760 | bytes 18726912 | tf_op jit(solution)/shard_map/dot_general | solution.py:408
  334.7 3.2 fusion.93
  338.4 4.5 fusion.8
  342.9 15.3 %scatter8.1 = f32[160,1152]{1,0:T(8,128)} custom-call(bf16[4,160,1152]{2,1,0:T(8,128)(2,1)} %bitcast.228), custom_call_target="tpu_custom_call" | custom-call | tf_op jit(solution)/shard_map/scatter8/pallas_call | solution.py:293
  362.1 13.0 %gather5.1 = bf16[4,160,1152]{2,1,0:T(8,128)(2,1)} custom-call(bf16[160,1152]{1,0:T(8,128)(2,1)} %multiply_convert_fusion.2.refs_0_), custom_call_target="tpu_custom_call" | custom-call | tf_op jit(solution)/shard_map/gather5/pallas_call | solution.py:167
  375.2 2.1 convolution_convert_fusion.10
  388.2 15.0 %scatter9.1 = f32[160,1152]{1,0:T(8,128)} custom-call(bf16[4,160,1152]{2,1,0:T(8,128)(2,1)} %bitcast.214), custom_call_target="tpu_custom_call" | custom-call | tf_op jit(solution)/shard_map/scatter9/pallas_call | solution.py:293
  404.7 2.3 fusion.38
  414.4 48.3 %scatter11.1 = (f32[144,256]{1,0:T(8,128)}, f32[144,256]{1,0:T(8,128)}, f32[16,256]{1,0:T(8,128)}, f32[144,256]{1,0:T(8,128)}, f32[144,256]{1,0:T(8,128)}) custom-call(bf16[8,144,256]{2,1,0:T(8,128)(2,1)} %bitcast.235, bf16[8,144,256]{2,1,0:T(8,128)(2,1)} %bitcast.236, bf16[8,16,256]{2,1,0:T(8,128)(2,1)} %pad.61.refs_2_, bf16[8,144,256]{2,1,0:T(8,128)(2,1)} %bitcast.237, ...), custom_call_target="tpu_custom_call" | custom-call | tf_op jit(solution)/shard_map/scatter11/pallas_call | solution.py:293
  465.4 7.0 %convolution_convert_fusion.2 = bf16[1152,1728]{0,1:T(8,128)(2,1)} fusion(bf16[640,1728]{0,1:T(8,128)(2,1)} %copy-done.62, bf16[640,1152]{1,0:T(8,128)(2,1)S(1)} %bitcast.222), kind=kOutput, calls=%fused_computation.2 | convolution fusion | flops 2550030336 | bytes 7667712 | tf_op jit(solution)/shard_map/dot_general | solution.py:65
  472.4 6.4 copy.41
  478.9 7.0 %convolution_convert_fusion.1 = bf16[1152,1728]{0,1:T(8,128)(2,1)} fusion(bf16[640,1728]{0,1:T(8,128)(2,1)} %copy-done.63, bf16[640,1152]{1,0:T(8,128)(2,1)S(1)} %bitcast.223), kind=kOutput, calls=%fused_computation.1 | convolution fusion | flops 2550030336 | bytes 7667712 | tf_op jit(solution)/shard_map/dot_general | solution.py:65
  485.9 6.5 copy.42
  492.4 7.0 %convolution_convert_fusion = bf16[1152,1728]{0,1:T(8,128)(2,1)} fusion(bf16[640,1728]{0,1:T(8,128)(2,1)} %copy-done.61, bf16[640,1152]{1,0:T(8,128)(2,1)S(1)} %bitcast.225), kind=kOutput, calls=%fused_computation | convolution fusion | flops 2550030336 | bytes 7667712 | tf_op jit(solution)/shard_map/dot_general | solution.py:65
  499.4 6.5 copy.43
  505.8 153.4 %scatter10.1 = (f32[144,1728]{1,0:T(8,128)}, f32[144,1728]{1,0:T(8,128)}, f32[144,1728]{1,0:T(8,128)}) custom-call(bf16[8,144,1728]{2,1,0:T(8,128)(2,1)} %bitcast.205, bf16[8,144,1728]{2,1,0:T(8,128)(2,1)} %bitcast.206, bf16[8,144,1728]{2,1,0:T(8,128)(2,1)} %bitcast.207), custom_call_target="tpu_custom_call" | custom-call | tf_op jit(solution)/shard_map/scatter10/pallas_call | solution.py:293
  661.9 2.3 copy.55
  (222 shorter events, 54.8 us)
Async XLA Ops:
  44.8 18.3 %copy-start.30 = (bf16[8,144,256]{2,1,0:T(8,128)(2,1)S(1)}, bf16[8,144,256]{2,1,0:T(8,128)(2,1)}, u32[]{:S(2)}) copy-start(bf16[8,144,256]{2,1,0:T(8,128)(2,1)} %get-tuple-element.32) | copy-start | bytes 1769476
  66.0 2.9 copy-start.53
  66.7 5.6 copy-start.3
  66.7 4.3 copy-start.12
  72.3 4.4 copy-start.5
  72.3 3.8 copy-start.24
  72.3 3.8 copy-start.46
  80.3 16.7 %copy-start.7 = (bf16[160,1152]{1,0:T(8,128)(2,1)S(1)}, bf16[160,1152]{1,0:T(8,128)(2,1)}, u32[]{:S(2)}) copy-start(bf16[160,1152]{1,0:T(8,128)(2,1)} %param.17) | copy-start | bytes 1105924
  273.6 6.6 copy-start.18
  273.6 6.6 copy-start.54
  280.2 6.7 %copy-start.60 = (f32[640,1728]{0,1:T(8,128)}, f32[640,1728]{0,1:T(8,128)S(1)}, u32[]{:S(2)}) copy-start(f32[640,1728]{0,1:T(8,128)S(1)} %fusion.92) | copy-start | bytes 13271044
  280.2 6.7 %copy-start.57 = (bf16[8,144,1728]{2,1,0:T(8,128)(2,1)S(1)}, bf16[8,144,1728]{2,1,0:T(8,128)(2,1)}, u32[]{:S(2)}) copy-start(bf16[8,144,1728]{2,1,0:T(8,128)(2,1)} %get-tuple-element.38) | copy-start | bytes 11943940
  286.9 4.5 copy-start.61
  291.4 15.5 %copy-start.44 = (f32[8,144]{1,0:T(8,128)S(1)}, f32[8,144]{1,0:T(8,128)}, u32[]{:S(2)}) copy-start(f32[8,144]{1,0:T(8,128)} %get-tuple-element.59) | copy-start | bytes 13828
  305.6 3.0 copy-start.2
  324.2 10.5 %copy-start.56 = (bf16[8,144,1728]{2,1,0:T(8,128)(2,1)S(1)}, bf16[8,144,1728]{2,1,0:T(8,128)(2,1)}, u32[]{:S(2)}) copy-start(bf16[8,144,1728]{2,1,0:T(8,128)(2,1)} %get-tuple-element.36) | copy-start | bytes 11943940
  334.6 3.2 copy-start.62
  334.7 3.2 copy-start.63
  334.7 3.8 copy-start.55
  342.9 16.8 %copy-start = (f32[160,1152]{1,0:T(8,128)S(1)}, f32[160,1152]{1,0:T(8,128)}, u32[]{:S(2)}) copy-start(f32[160,1152]{1,0:T(8,128)} %scatter6.1) | copy-start | bytes 2211844
  342.9 16.8 %copy-start.11 = (bf16[160,1152]{1,0:T(8,128)(2,1)S(1)}, bf16[160,1152]{1,0:T(8,128)(2,1)}, u32[]{:S(2)}) copy-start(bf16[160,1152]{1,0:T(8,128)(2,1)} %param.31) | copy-start | bytes 1105924
  361.2 14.0 %copy-start.33 = (bf16[8,144,256]{2,1,0:T(8,128)(2,1)S(1)}, bf16[8,144,256]{2,1,0:T(8,128)(2,1)}, u32[]{:S(2)}) copy-start(bf16[8,144,256]{2,1,0:T(8,128)(2,1)} %get-tuple-element.35) | copy-start | bytes 1769476
  388.2 15.1 %copy-start.48 = (f32[160]{0:T(256)S(1)}, f32[160]{0:T(256)}, u32[]{:S(2)}) copy-start(f32[160]{0:T(256)} %copy-done.47) | copy-start | bytes 1924
  388.2 16.5 %copy-start.9 = (f32[160,1152]{1,0:T(8,128)S(1)}, f32[160,1152]{1,0:T(8,128)}, u32[]{:S(2)}) copy-start(f32[160,1152]{1,0:T(8,128)} %copy-done.8) | copy-start | bytes 2211844
  414.4 51.0 %copy-start.19 = (bf16[4,160,1152]{2,1,0:T(8,128)(2,1)S(1)}, bf16[4,160,1152]{2,1,0:T(8,128)(2,1)}, u32[]{:S(2)}) copy-start(bf16[4,160,1152]{2,1,0:T(8,128)(2,1)} %gather3.1) | copy-start | bytes 4423684
  485.9 6.5 copy-start.20
  505.8 153.4 %copy-start.39 = (f32[144,256]{1,0:T(8,128)S(1)}, f32[144,256]{1,0:T(8,128)}, u32[]{:S(2)}) copy-start(f32[144,256]{1,0:T(8,128)} %get-tuple-element.122) | copy-start | bytes 442372
  505.8 154.1 %copy-start.38 = (f32[144,256]{1,0:T(8,128)S(1)}, f32[144,256]{1,0:T(8,128)}, u32[]{:S(2)}) copy-start(f32[144,256]{1,0:T(8,128)} %get-tuple-element.123) | copy-start | bytes 442372
  505.8 154.7 %copy-start.37 = (f32[144,256]{1,0:T(8,128)S(1)}, f32[144,256]{1,0:T(8,128)}, u32[]{:S(2)}) copy-start(f32[144,256]{1,0:T(8,128)} %get-tuple-element.124) | copy-start | bytes 442372
  505.8 155.4 %copy-start.36 = (f32[144,256]{1,0:T(8,128)S(1)}, f32[144,256]{1,0:T(8,128)}, u32[]{:S(2)}) copy-start(f32[144,256]{1,0:T(8,128)} %get-tuple-element.43) | copy-start | bytes 442372
  659.2 5.0 copy-start.23
  661.9 3.3 copy-start.22
  (32 other events, 49.3 us)

commit v2 on v1

--- a/solution.py
+++ b/solution.py
@@ -76,6 +76,7 @@
 MESH = pl.DeviceIdType.MESH
 LANES = 128
 SUBLANES = 16
+MICROSECOND = 3_600_000
 
 
 def pieces_of(shapes, wanted):
@@ -159,7 +160,7 @@
             near(c, k).wait()
 
 
-def gather(axis, n, arrays, wanted, ident):
+def gather(axis, n, arrays, wanted, ident, cost):
     shapes = [array.shape for array in arrays]
     pieces = pieces_of(shapes, wanted)
     count = len(arrays)
@@ -171,6 +172,7 @@
         out_specs=[pl.BlockSpec(memory_space=pl.ANY)] * count,
         scratch_shapes=[pltpu.SemaphoreType.DMA((count,)), sems, sems, sems, sems],
         compiler_params=pltpu.CompilerParams(collective_id=ident, has_side_effects=True),
+        cost_estimate=pl.CostEstimate(flops=0, bytes_accessed=cost * MICROSECOND, transcendentals=0),
         name=f"gather{ident}",
     )(*arrays)
 
@@ -283,7 +285,7 @@
                 far(c, k).wait_send()
 
 
-def scatter(axis, n, arrays, wanted, ident, shared=(), other=None, n_other=1):
+def scatter(axis, n, arrays, wanted, ident, cost, shared=(), other=None, n_other=1):
     shapes = [array.shape[1:] for array in arrays]
     pieces = pieces_of(shapes, wanted)
     count = len(arrays)
@@ -303,6 +305,7 @@
         compiler_params=pltpu.CompilerParams(
             collective_id=ident, has_side_effects=True, vmem_limit_bytes=60 * 1024 * 1024
         ),
+        cost_estimate=pl.CostEstimate(flops=0, bytes_accessed=cost * MICROSECOND, transcendentals=0),
         name=f"scatter{ident}",
     )(*arrays)
 
@@ -340,7 +343,7 @@
     width = -(-max(gain.shape[0] for gain in gains) // LANES) * LANES
     gain_rows = pack_gains([gain[None] for gain in gains], width)[0]
     attn_full = gather(
-        "dp", n_dp, [gain_rows, w_query, w_key, w_value, w_output.T], 1, 0
+        "dp", n_dp, [gain_rows, w_query, w_key, w_value, w_output.T], 1, 0, 36
     )
     full_in_gain, full_attn_gain, full_ffn_gain, full_out_gain, full_qgain, full_kgain = (
         attn_full[0][:, row, : gain.shape[0]].reshape(-1) for row, gain in enumerate(gains)
@@ -351,7 +354,7 @@
     heads_local = full_query.shape[1] // HD
     hidden_f = hidden.astype(jnp.float32)
     normed_local = apply_norm(hidden_f, full_in_gain).astype(jnp.bfloat16)
-    normed_in = gather("tensor", n_tensor, [normed_local], 2, 2)[0].reshape(-1, normed_local.shape[-1])
+    normed_in = gather("tensor", n_tensor, [normed_local], 5, 2, 13)[0].reshape(-1, normed_local.shape[-1])
     seq_len = normed_in.shape[0]
     query_raw = jnp.dot(normed_in, full_query, preferred_element_type=jnp.float32).reshape(
         seq_len, heads_local, HD
@@ -378,16 +381,16 @@
         "tensor",
         n_tensor,
         [attn_part.astype(jnp.bfloat16).reshape(n_tensor, -1, attn_part.shape[-1])],
-        2,
+        5,
         6,
+        14,
     )[0]
     residual = hidden_f + apply_norm(attn_rows, full_attn_gain)
-    full_gate, full_up, full_down = (
-        block.reshape(-1, block.shape[-1])
-        for block in gather("dp", n_dp, [w_gate, w_up, w_down.T], 3, 1)
-    )
+    full_gate = lax.all_gather(w_gate, "dp", axis=0, tiled=True)
+    full_up = lax.all_gather(w_up, "dp", axis=0, tiled=True)
+    full_down = gather("dp", n_dp, [w_down.T], 9, 1, 55)[0].reshape(-1, w_down.shape[0])
     ffn_local = apply_norm(residual, full_ffn_gain).astype(jnp.bfloat16)
-    ffn_in = gather("tensor", n_tensor, [ffn_local], 2, 3)[0].reshape(-1, ffn_local.shape[-1])
+    ffn_in = gather("tensor", n_tensor, [ffn_local], 5, 3, 13)[0].reshape(-1, ffn_local.shape[-1])
     gate_pre = jnp.dot(ffn_in, full_gate, preferred_element_type=jnp.float32)
     up_pre = jnp.dot(ffn_in, full_up, preferred_element_type=jnp.float32)
     gelu_values, gelu_back = jax.vjp(gelu_tanh, gate_pre)
@@ -397,13 +400,14 @@
         "tensor",
         n_tensor,
         [down_part.astype(jnp.bfloat16).reshape(n_tensor, -1, down_part.shape[-1])],
-        2,
+        5,
         7,
+        14,
     )[0]
     output = (residual + apply_norm(down_rows, full_out_gain)).astype(jnp.bfloat16)
     cot_f = cotangent.astype(jnp.float32)
     grad_down, term_out = norm_back(down_rows, full_out_gain, cot_f)
-    down_all = gather("tensor", n_tensor, [grad_down.astype(jnp.bfloat16)], 2, 4)[0].reshape(-1, grad_down.shape[-1])
+    down_all = gather("tensor", n_tensor, [grad_down.astype(jnp.bfloat16)], 5, 4, 13)[0].reshape(-1, grad_down.shape[-1])
     grad_wd = contract_rows(down_all, mixed)
     grad_mixed = jnp.dot(down_all, full_down, preferred_element_type=jnp.float32)
     gate_low = gelu_back(grad_mixed * up_pre)[0].astype(jnp.bfloat16)
@@ -415,13 +419,14 @@
         "tensor",
         n_tensor,
         [ffn_part.astype(jnp.bfloat16).reshape(n_tensor, -1, ffn_part.shape[-1])],
-        2,
+        5,
         8,
+        14,
     )[0]
     resid_norm, term_ffn = norm_back(residual, full_ffn_gain, ffn_back)
     grad_residual = cot_f + resid_norm
     grad_attn, term_attn = norm_back(attn_rows, full_attn_gain, grad_residual)
-    attn_all = gather("tensor", n_tensor, [grad_attn.astype(jnp.bfloat16)], 2, 5)[0].reshape(-1, grad_attn.shape[-1])
+    attn_all = gather("tensor", n_tensor, [grad_attn.astype(jnp.bfloat16)], 5, 5, 13)[0].reshape(-1, grad_attn.shape[-1])
     grad_wo = contract_rows(attn_all, context)
     grad_context = (
         jnp.dot(attn_all, full_output, preferred_element_type=jnp.float32)
@@ -468,17 +473,22 @@
         "tensor",
         n_tensor,
         [attn_in_part.astype(jnp.bfloat16).reshape(n_tensor, -1, attn_in_part.shape[-1])],
-        2,
+        5,
         9,
+        14,
     )[0]
     in_norm, term_in = norm_back(hidden_f, full_in_gain, attn_back)
     grad_hidden = grad_residual + in_norm
     def blocks(values):
         return values.astype(jnp.bfloat16).reshape(n_dp, -1, values.shape[-1])
 
-    ffn_grads = scatter(
-        "dp", n_dp, [blocks(grad_wg), blocks(grad_wu), blocks(grad_wd)], 3, 10
-    )
+    own_gate, own_down = (
+        lax.psum_scatter(
+            grad.astype(jnp.bfloat16), "dp", scatter_dimension=0, tiled=True
+        ).astype(jnp.float32)
+        for grad in (grad_wg, grad_wd)
+    )
+    own_up = scatter("dp", n_dp, [blocks(grad_wu)], 9, 10, 52)[0]
     gain_grads = [
         jnp.sum(term, axis=tuple(range(term.ndim - 1))).astype(jnp.bfloat16).reshape(n_dp, -1)
         for term in (term_in, term_attn, term_ffn, term_out, term_qgain, term_kgain)
@@ -495,6 +505,7 @@
         ],
         1,
         11,
+        46,
         shared=(0, 1, 2),
         other="tensor",
         n_other=n_tensor,
@@ -514,9 +525,9 @@
         attn_grads[4].T,
         own_attn,
         own_ffn,
-        ffn_grads[0],
-        ffn_grads[1],
-        ffn_grads[2].T,
+        own_gate,
+        own_up,
+        own_down.T,
         own_out,
     )
 

time: 673 us -> 555 us (0.82)
  Pallas kernels: 516 us -> 397 us
  local copies, waits for them, and re-layouts: 41.3 us -> 25.7 us
  between operations: 2 us -> 14.9 us
    pallas_call x6, Pallas kernels: 262 us -> 199 us  [scatter(): pl.pallas_call(functools.partial(scatter_body, axis, n, pieces, count, sh...]
    pallas_call x6, Pallas kernels: 254 us -> 198 us  [gather(): pl.pallas_call(functools.partial(gather_body, axis, n, pieces, count), ou...]
    convert_element_type x3 -> x1, local copies, waits for them, and re-layouts: 19.4 us -> 6.44 us  [blocks(): return values.astype(jnp.bfloat16).reshape(n_dp, -1, values.shape[-1])]
  transfers between devices with their start and end apart: 0 -> 4, of which waited for: 0 -> 0; matrix products, arithmetic and copies ran while one was open for 0% -> 17% of each run, Pallas kernels for 0% -> 67%
where the time goes in v2:
time: 555 us; the launch traced here: 548 us
  Pallas kernels  397 us (72%)
  matrix products  82.8 us (15%)
  other arithmetic  26.4 us (5%)
  local copies, waits for them, and re-layouts  25.7 us (5%)
  between operations  14.9 us (3%)
    pallas_call x6, Pallas kernels, scatter(): pl.pallas_call(functools.partial(scatter_body, axis, n, pieces, count, sh...  199 us
    pallas_call x6, Pallas kernels, gather(): pl.pallas_call(functools.partial(gather_body, axis, n, pieces, count), ou...  198 us
    dot_general x5, matrix products, contract_rows(): lax.dot_general(left, right, (((0,), (0,)), ((), ())), preferred_element_...  22.5 us
    dot_general x5, matrix products, contract_cols(): lax.dot_general(left, right, (((1,), (1,)), ((), ())), preferred_element_...  14.8 us
  transfers between devices with their start and end apart: 4, of which 0 were waited for; matrix products, arithmetic and copies ran while one was open for 17% of the time, Pallas kernels for 67%

profile of v2, /device:TPU:0, one launch (start us, length us, event | category | flops | bytes accessed | tf_op | source)
XLA Modules:
  0.0 548.3 jit_solution(9287159465364825305)
XLA Ops:
  12.7 54.9 %gather0.1 = (bf16[8,16,256]{2,1,0:T(8,128)(2,1)}, bf16[8,144,256]{2,1,0:T(8,128)(2,1)}, bf16[8,144,256]{2,1,0:T(8,128)(2,1)}, bf16[8,144,256]{2,1,0:T(8,128)(2,1)}, bf16[8,144,256]{2,1,0:T(8,128)(2,1)}) custom-call(bf16[16,256]{1,0:T(8,128)(2,1)} %pad_bitcast_fusion.refs_0_, bf16[144,256]{1,0:T(8,128)(2,1)} %refs_1_.1, bf16[144,256]{1,0:T(8,128)(2,1)} %refs_2_.1, ...), custom_call_target="tpu_custom_call" | custom-call | bytes 129600000 | tf_op jit(solution)/shard_map/gather0/pallas_call | solution.py:168
  69.9 13.5 %gather2.1 = bf16[4,160,1152]{2,1,0:T(8,128)(2,1)} custom-call(bf16[160,1152]{1,0:T(8,128)(2,1)} %fusion.34.refs_0_), custom_call_target="tpu_custom_call" | custom-call | bytes 46800000 | tf_op jit(solution)/shard_map/gather2/pallas_call | solution.py:168
  84.4 2.1 multiply_reduce_fusion.12
  93.6 1.8 convolution_convert_fusion.3
  95.4 15.0 %scatter6.1 = f32[160,1152]{1,0:T(8,128)} custom-call(bf16[4,160,1152]{2,1,0:T(8,128)(2,1)} %bitcast.210), custom_call_target="tpu_custom_call" | custom-call | bytes 50400000 | tf_op jit(solution)/shard_map/scatter6/pallas_call | solution.py:295
  114.1 13.0 %gather3.1 = bf16[4,160,1152]{2,1,0:T(8,128)(2,1)} custom-call(bf16[160,1152]{1,0:T(8,128)(2,1)} %multiply_convert_fusion.3.refs_0_), custom_call_target="tpu_custom_call" | custom-call | bytes 46800000 | tf_op jit(solution)/shard_map/gather3/pallas_call | solution.py:168
  127.2 89.9 %gather1.1 = bf16[8,144,1728]{2,1,0:T(8,128)(2,1)} custom-call(bf16[144,1728]{1,0:T(8,128)(2,1)} %bitcast.235), custom_call_target="tpu_custom_call" | custom-call | bytes 198000000 | tf_op jit(solution)/shard_map/gather1/pallas_call | solution.py:168
  217.2 8.2 %fusion.92 = f32[640,1728]{0,1:T(8,128)} fusion(bf16[640,1152]{1,0:T(8,128)(2,1)} %bitcast.217, bf16[1152,1728]{1,0:T(8,128)(2,1)} %all-gather.3.cloned.1.call-done), kind=kOutput, calls=%fused_computation.189 | convolution fusion | flops 2548039680 | bytes 9879552 | tf_op jit(solution)/shard_map/dot_general | solution.py:394
  225.4 10.7 %multiply_convert_fusion.1 = (bf16[640,1728]{0,1:T(8,128)(2,1)S(1)}, f32[640,1728]{0,1:T(8,128)}) fusion(f32[640,1728]{0,1:T(8,128)} %fusion.92, bf16[640,1152]{1,0:T(8,128)(2,1)} %bitcast.218, bf16[1152,1728]{1,0:T(8,128)(2,1)} %all-gather.5.cloned.1.call-done), kind=kOutput, calls=%fused_computation.13 | convolution fusion | flops 2559098880 | bytes 16515072 | tf_op jit(solution)/shard_map/dot_general | solution.py:395
  236.1 4.7 convolution_convert_fusion.4
  240.8 14.8 %scatter7.1 = f32[160,1152]{1,0:T(8,128)} custom-call(bf16[4,160,1152]{2,1,0:T(8,128)(2,1)} %bitcast.226), custom_call_target="tpu_custom_call" | custom-call | bytes 50400000 | tf_op jit(solution)/shard_map/scatter7/pallas_call | solution.py:295
  259.6 13.2 %gather4.1 = bf16[4,160,1152]{2,1,0:T(8,128)(2,1)} custom-call(bf16[160,1152]{1,0:T(8,128)(2,1)} %get-tuple-element.58.refs_0_), custom_call_target="tpu_custom_call" | custom-call | bytes 46800000 | tf_op jit(solution)/shard_map/gather4/pallas_call | solution.py:168
  272.8 7.5 %convolution_convert_fusion.1 = bf16[1152,1728]{1,0:T(8,128)(2,1)} fusion(bf16[640,1152]{1,0:T(8,128)(2,1)} %bitcast.223, bf16[640,1728]{0,1:T(8,128)(2,1)} %copy-done.55), kind=kOutput, calls=%fused_computation.1 | convolution fusion | flops 2550030336 | bytes 7667712 | tf_op jit(solution)/shard_map/dot_general | solution.py:65
  280.3 10.5 %multiply_convert_fusion = (bf16[640,1728]{0,1:T(8,128)(2,1)S(1)}, bf16[640,1728]{0,1:T(8,128)(2,1)S(1)}) fusion(f32[640,1728]{0,1:T(8,128)} %fusion.92, f32[640,1728]{0,1:T(8,128)} %get-tuple-element.83, bf16[640,1152]{1,0:T(8,128)(2,1)} %bitcast.224, bf16[1152,1728]{1,0:T(8,128)(2,1)} %bitcast.211), kind=kOutput, calls=%fused_computation.12 | convolution fusion | flops 2574581760 | bytes 18726912 | tf_op jit(solution)/shard_map/dot_general | solution.py:412
  290.9 3.2 fusion.93
  294.6 4.5 fusion.8
  299.1 15.1 %scatter8.1 = f32[160,1152]{1,0:T(8,128)} custom-call(bf16[4,160,1152]{2,1,0:T(8,128)(2,1)} %bitcast.225), custom_call_target="tpu_custom_call" | custom-call | bytes 50400000 | tf_op jit(solution)/shard_map/scatter8/pallas_call | solution.py:295
  314.2 1.5 multiply_reduce_fusion
  318.1 13.2 %gather5.1 = bf16[4,160,1152]{2,1,0:T(8,128)(2,1)} custom-call(bf16[160,1152]{1,0:T(8,128)(2,1)} %multiply_convert_fusion.2.refs_0_), custom_call_target="tpu_custom_call" | custom-call | bytes 46800000 | tf_op jit(solution)/shard_map/gather5/pallas_call | solution.py:168
  331.3 2.9 convolution_convert_fusion.10
  334.1 7.0 %convolution_convert_fusion.2 = bf16[1152,1728]{1,0:T(8,128)(2,1)} fusion(bf16[640,1152]{1,0:T(8,128)(2,1)S(1)} %bitcast.219, bf16[640,1728]{0,1:T(8,128)(2,1)} %copy-done.56), kind=kOutput, calls=%fused_computation.2 | convolution fusion | flops 2550030336 | bytes 7667712 | tf_op jit(solution)/shard_map/dot_general | solution.py:65
  342.6 1.7 fusion.9
  353.2 1.8 fusion.7
  355.0 15.1 %scatter9.1 = f32[160,1152]{1,0:T(8,128)} custom-call(bf16[4,160,1152]{2,1,0:T(8,128)(2,1)} %bitcast.209), custom_call_target="tpu_custom_call" | custom-call | bytes 50400000 | tf_op jit(solution)/shard_map/scatter9/pallas_call | solution.py:295
  373.0 1.5 convolution_convert_fusion.7
  377.4 1.5 convolution_convert_fusion.5
  378.9 72.2 %scatter11.1 = (f32[144,256]{1,0:T(8,128)}, f32[144,256]{1,0:T(8,128)}, f32[16,256]{1,0:T(8,128)}, f32[144,256]{1,0:T(8,128)}, f32[144,256]{1,0:T(8,128)}) custom-call(bf16[8,144,256]{2,1,0:T(8,128)(2,1)} %bitcast.232, bf16[8,144,256]{2,1,0:T(8,128)(2,1)} %bitcast.231, bf16[8,16,256]{2,1,0:T(8,128)(2,1)} %pad.61.refs_2_, bf16[8,144,256]{2,1,0:T(8,128)(2,1)} %bitcast.233, ...), custom_call_target="tpu_custom_call" | custom-call | bytes 165600000 | tf_op jit(solution)/shard_map/scatter11/pallas_call | solution.py:295
  451.1 5.0 convolution_convert_fusion
  456.1 6.4 %copy.39 = bf16[1152,1728]{1,0:T(8,128)(2,1)} copy(bf16[1152,1728]{0,1:T(8,128)(2,1)} %convolution_convert_fusion) | data formatting | bytes 7962624 | tf_op jit(solution)/shard_map/convert_element_type | solution.py:483
  462.6 67.1 %scatter10.1 = f32[144,1728]{1,0:T(8,128)} custom-call(bf16[8,144,1728]{2,1,0:T(8,128)(2,1)} %bitcast.202), custom_call_target="tpu_custom_call" | custom-call | bytes 187200000 | tf_op jit(solution)/shard_map/scatter10/pallas_call | solution.py:295
  533.6 2.1 convert_bitcast_fusion
  535.7 2.2 convert_element_type.312
  (222 shorter events, 49.9 us)
Async XLA Ops:
  7.2 61.6 %copy-start.7 = (bf16[160,1152]{1,0:T(8,128)(2,1)S(1)}, bf16[160,1152]{1,0:T(8,128)(2,1)}, u32[]{:S(2)}) copy-start(bf16[160,1152]{1,0:T(8,128)(2,1)} %param.17) | copy-start | bytes 1105924
  7.2 210.0 %all-gather.3.cloned.1.call-start = ((), (), s32[]{:S(2)}) async-start(), calls=%async_computation.2 | async-start | bytes 4644864 | tf_op jit(solution)/shard_map/all_gather | solution.py:389
  7.9 217.5 %all-gather.5.cloned.1.call-start = ((), (), s32[]{:S(2)}) async-start(), calls=%async_computation.3 | async-start | bytes 4644864 | tf_op jit(solution)/shard_map/all_gather | solution.py:390
  8.7 524.9 %reduce-scatter.5.cloned.1.call-start = ((), (), s32[]{:S(2)}) async-start(), calls=%async_computation.5 | async-start | bytes 4644864 | tf_op jit(solution)/shard_map/reduce_scatter | solution.py:486
  12.7 71.7 %copy-start.50 = (s32[640]{0:T(1024)S(1)}, s32[640]{0:T(1024)}, u32[]{:S(2)}) copy-start(s32[640]{0:T(1024)} %param.33) | copy-start | bytes 7684
  67.6 16.8 %copy-start.16 = (bf16[8,144,256]{2,1,0:T(8,128)(2,1)S(1)}, bf16[8,144,256]{2,1,0:T(8,128)(2,1)}, u32[]{:S(2)}) copy-start(bf16[8,144,256]{2,1,0:T(8,128)(2,1)} %get-tuple-element.27) | copy-start | bytes 1769476
  83.3 3.3 copy-start.1
  83.3 3.3 copy-start.18
  87.5 3.1 copy-start.49
  225.4 10.7 %copy-start.12 = (bf16[8,144,1728]{2,1,0:T(8,128)(2,1)S(1)}, bf16[8,144,1728]{2,1,0:T(8,128)(2,1)}, u32[]{:S(2)}) copy-start(bf16[8,144,1728]{2,1,0:T(8,128)(2,1)} %gather1.1) | copy-start | bytes 11943940
  236.0 4.7 copy-start.55
  240.8 16.2 %copy-start.14 = (bf16[160,1152]{1,0:T(8,128)(2,1)S(1)}, bf16[160,1152]{1,0:T(8,128)(2,1)}, u32[]{:S(2)}) copy-start(bf16[160,1152]{1,0:T(8,128)(2,1)} %param.31) | copy-start | bytes 1105924
  280.3 255.4 %reduce-scatter.3.cloned.1.call-start = ((), (), s32[]{:S(2)}) async-start(), calls=%async_computation.4 | async-start | bytes 4644864 | tf_op jit(solution)/shard_map/reduce_scatter | solution.py:486
  280.3 10.5 %copy-start.51 = (bf16[1152,1728]{1,0:T(8,128)(2,1)S(1)}, bf16[1152,1728]{1,0:T(8,128)(2,1)}, u32[]{:S(2)}) copy-start(bf16[1152,1728]{1,0:T(8,128)(2,1)} %all-gather.3.cloned.1.call-done) | copy-start | bytes 11943940
  290.8 3.2 copy-start.56
  290.8 3.2 copy-start.57
  290.8 3.8 copy-start.52
  299.1 16.6 %copy-start = (f32[160,1152]{1,0:T(8,128)S(1)}, f32[160,1152]{1,0:T(8,128)}, u32[]{:S(2)}) copy-start(f32[160,1152]{1,0:T(8,128)} %scatter6.1) | copy-start | bytes 2211844
  299.1 16.6 %copy-start.15 = (bf16[160,1152]{1,0:T(8,128)(2,1)S(1)}, bf16[160,1152]{1,0:T(8,128)(2,1)}, u32[]{:S(2)}) copy-start(bf16[160,1152]{1,0:T(8,128)(2,1)} %param.31) | copy-start | bytes 1105924
  317.1 14.1 %copy-start.40 = (bf16[8,144,256]{2,1,0:T(8,128)(2,1)S(1)}, bf16[8,144,256]{2,1,0:T(8,128)(2,1)}, u32[]{:S(2)}) copy-start(bf16[8,144,256]{2,1,0:T(8,128)(2,1)} %get-tuple-element.29) | copy-start | bytes 1769476
  331.3 2.9 copy-start.22
  355.0 18.0 %copy-start.44 = (bf16[640,256]{0,1:T(8,128)(2,1)S(1)}, bf16[640,256]{0,1:T(8,128)(2,1)}, u32[]{:S(2)}) copy-start(bf16[640,256]{0,1:T(8,128)(2,1)} %copy-done.43) | copy-start | bytes 983044
  371.5 2.9 copy-start.26
  377.4 73.7 %copy-start.58 = (bf16[640,1728]{0,1:T(8,128)(2,1)S(1)}, bf16[640,1728]{0,1:T(8,128)(2,1)}, u32[]{:S(2)}) copy-start(bf16[640,1728]{0,1:T(8,128)(2,1)} %copy-done.57) | copy-start | bytes 6635524
  378.9 72.2 %copy-start.23 = (bf16[4,160,1152]{2,1,0:T(8,128)(2,1)S(1)}, bf16[4,160,1152]{2,1,0:T(8,128)(2,1)}, u32[]{:S(2)}) copy-start(bf16[4,160,1152]{2,1,0:T(8,128)(2,1)} %gather3.1) | copy-start | bytes 4423684
  462.6 69.9 %copy-start.9 = (f32[160,1152]{1,0:T(8,128)S(1)}, f32[160,1152]{1,0:T(8,128)}, u32[]{:S(2)}) copy-start(f32[160,1152]{1,0:T(8,128)} %copy-done.8) | copy-start | bytes 2211844
  462.6 69.9 %copy-start.10 = (f32[160,1152]{1,0:T(8,128)S(1)}, f32[160,1152]{1,0:T(8,128)}, u32[]{:S(2)}) copy-start(f32[160,1152]{1,0:T(8,128)} %scatter9.1) | copy-start | bytes 2211844
  533.6 4.3 copy-start.48
  533.6 5.0 copy-start.47
  533.6 5.6 %copy-start.46 = (f32[144,256]{1,0:T(8,128)S(1)}, f32[144,256]{1,0:T(8,128)}, u32[]{:S(2)}) copy-start(f32[144,256]{1,0:T(8,128)} %get-tuple-element.112) | copy-start | bytes 442372
  533.6 6.3 %copy-start.45 = (f32[144,256]{1,0:T(8,128)S(1)}, f32[144,256]{1,0:T(8,128)}, u32[]{:S(2)}) copy-start(f32[144,256]{1,0:T(8,128)} %get-tuple-element.34) | copy-start | bytes 442372
  535.7 4.8 copy-start.13
  (31 other events, 43.4 us)
Sparse Core Ops, SparseCore 0:
  10.2 94.3 all-gather.2
  106.8 103.3 all-gather.4
  280.4 88.1 reduce-scatter.4
  372.0 124.2 reduce-scatter.2

commit v3 on v2

--- a/solution.py
+++ b/solution.py
@@ -488,7 +488,6 @@
         ).astype(jnp.float32)
         for grad in (grad_wg, grad_wd)
     )
-    own_up = scatter("dp", n_dp, [blocks(grad_wu)], 9, 10, 52)[0]
     gain_grads = [
         jnp.sum(term, axis=tuple(range(term.ndim - 1))).astype(jnp.bfloat16).reshape(n_dp, -1)
         for term in (term_in, term_attn, term_ffn, term_out, term_qgain, term_kgain)
@@ -502,10 +501,11 @@
             pack_gains(gain_grads, width),
             blocks(grad_wq),
             blocks(grad_wo),
+            blocks(grad_wu),
         ],
-        1,
+        3,
         11,
-        46,
+        100,
         shared=(0, 1, 2),
         other="tensor",
         n_other=n_tensor,
@@ -526,7 +526,7 @@
         own_attn,
         own_ffn,
         own_gate,
-        own_up,
+        attn_grads[5],
         own_down.T,
         own_out,
     )

time: 555 us -> 538 us (0.969)
  Pallas kernels: 397 us -> 374 us
    pallas_call x6 -> x5, Pallas kernels: 199 us -> 176 us  [scatter(): pl.pallas_call(functools.partial(scatter_body, axis, n, pieces, count, sh...]
  transfers between devices with their start and end apart: 4 -> 4, of which waited for: 0 -> 0; matrix products, arithmetic and copies ran while one was open for 17% -> 17% of each run, Pallas kernels for 67% -> 66%
where the time goes in v3:
time: 538 us; the launch traced here: 527 us
  Pallas kernels  374 us (70%)
  matrix products  84.4 us (16%)
  other arithmetic  26.4 us (5%)
  local copies, waits for them, and re-layouts  25.9 us (5%)
  between operations  14.9 us (3%)
    pallas_call x6, Pallas kernels, gather(): pl.pallas_call(functools.partial(gather_body, axis, n, pieces, count), ou...  198 us
    pallas_call x5, Pallas kernels, scatter(): pl.pallas_call(functools.partial(scatter_body, axis, n, pieces, count, sh...  176 us
    dot_general x5, matrix products, contract_rows(): lax.dot_general(left, right, (((0,), (0,)), ((), ())), preferred_element_...  22.5 us
    dot_general x5, matrix products, contract_cols(): lax.dot_general(left, right, (((1,), (1,)), ((), ())), preferred_element_...  17.7 us
    dot_general x1, matrix products, local(): jnp.dot(down_all, full_down, preferred_element_type=jnp.float32)  11.4 us
    unnamed x125, local copies, waits for them, and re-layouts  10.9 us
  transfers between devices with their start and end apart: 4, of which 0 were waited for; matrix products, arithmetic and copies ran while one was open for 17% of the time, Pallas kernels for 66%

profile of v3, /device:TPU:0, one launch (start us, length us, event | category | flops | bytes accessed | tf_op | source)
XLA Modules:
  0.0 527.4 jit_solution(14609369113414051552)
XLA Ops:
  12.7 54.9 %gather0.1 = (bf16[8,16,256]{2,1,0:T(8,128)(2,1)}, bf16[8,144,256]{2,1,0:T(8,128)(2,1)}, bf16[8,144,256]{2,1,0:T(8,128)(2,1)}, bf16[8,144,256]{2,1,0:T(8,128)(2,1)}, bf16[8,144,256]{2,1,0:T(8,128)(2,1)}) custom-call(bf16[16,256]{1,0:T(8,128)(2,1)} %pad_bitcast_fusion.refs_0_, bf16[144,256]{1,0:T(8,128)(2,1)} %refs_1_.1, bf16[144,256]{1,0:T(8,128)(2,1)} %refs_2_.1, ...), custom_call_target="tpu_custom_call" | custom-call | bytes 129600000 | tf_op jit(solution)/shard_map/gather0/pallas_call | solution.py:168
  69.9 13.5 %gather2.1 = bf16[4,160,1152]{2,1,0:T(8,128)(2,1)} custom-call(bf16[160,1152]{1,0:T(8,128)(2,1)} %fusion.34.refs_0_), custom_call_target="tpu_custom_call" | custom-call | bytes 46800000 | tf_op jit(solution)/shard_map/gather2/pallas_call | solution.py:168
  84.5 2.1 multiply_reduce_fusion.11
  93.7 1.8 convolution_convert_fusion.3
  95.5 15.0 %scatter6.1 = f32[160,1152]{1,0:T(8,128)} custom-call(bf16[4,160,1152]{2,1,0:T(8,128)(2,1)} %bitcast.210), custom_call_target="tpu_custom_call" | custom-call | bytes 50400000 | tf_op jit(solution)/shard_map/scatter6/pallas_call | solution.py:295
  114.1 13.0 %gather3.1 = bf16[4,160,1152]{2,1,0:T(8,128)(2,1)} custom-call(bf16[160,1152]{1,0:T(8,128)(2,1)} %multiply_convert_fusion.3.refs_0_), custom_call_target="tpu_custom_call" | custom-call | bytes 46800000 | tf_op jit(solution)/shard_map/gather3/pallas_call | solution.py:168
  127.2 89.9 %gather1.1 = bf16[8,144,1728]{2,1,0:T(8,128)(2,1)} custom-call(bf16[144,1728]{1,0:T(8,128)(2,1)} %bitcast.235), custom_call_target="tpu_custom_call" | custom-call | bytes 198000000 | tf_op jit(solution)/shard_map/gather1/pallas_call | solution.py:168
  217.2 8.2 %fusion.92 = f32[640,1728]{0,1:T(8,128)} fusion(bf16[640,1152]{1,0:T(8,128)(2,1)} %bitcast.217, bf16[1152,1728]{1,0:T(8,128)(2,1)} %all-gather.3.cloned.1.call-done), kind=kOutput, calls=%fused_computation.189 | convolution fusion | flops 2548039680 | bytes 9879552 | tf_op jit(solution)/shard_map/dot_general | solution.py:394
  225.4 10.7 %multiply_convert_fusion.1 = (bf16[640,1728]{0,1:T(8,128)(2,1)S(1)}, f32[640,1728]{0,1:T(8,128)}) fusion(f32[640,1728]{0,1:T(8,128)} %fusion.92, bf16[640,1152]{1,0:T(8,128)(2,1)} %bitcast.218, bf16[1152,1728]{1,0:T(8,128)(2,1)} %all-gather.5.cloned.1.call-done), kind=kOutput, calls=%fused_computation.13 | convolution fusion | flops 2559098880 | bytes 16515072 | tf_op jit(solution)/shard_map/dot_general | solution.py:395
  236.1 4.8 convolution_convert_fusion.4
  240.9 14.9 %scatter7.1 = f32[160,1152]{1,0:T(8,128)} custom-call(bf16[4,160,1152]{2,1,0:T(8,128)(2,1)} %bitcast.226), custom_call_target="tpu_custom_call" | custom-call | bytes 50400000 | tf_op jit(solution)/shard_map/scatter7/pallas_call | solution.py:295
  259.7 13.2 %gather4.1 = bf16[4,160,1152]{2,1,0:T(8,128)(2,1)} custom-call(bf16[160,1152]{1,0:T(8,128)(2,1)} %get-tuple-element.60.refs_0_), custom_call_target="tpu_custom_call" | custom-call | bytes 46800000 | tf_op jit(solution)/shard_map/gather4/pallas_call | solution.py:168
  272.9 11.4 %multiply_convert_fusion = (bf16[640,1728]{0,1:T(8,128)(2,1)}, bf16[640,1728]{0,1:T(8,128)(2,1)S(1)}) fusion(f32[640,1728]{0,1:T(8,128)} %fusion.92, f32[640,1728]{0,1:T(8,128)} %get-tuple-element.85, bf16[640,1152]{1,0:T(8,128)(2,1)} %bitcast.223, bf16[1152,1728]{1,0:T(8,128)(2,1)} %bitcast.211), kind=kOutput, calls=%fused_computation.12 | convolution fusion | flops 2574581760 | bytes 18726912 | tf_op jit(solution)/shard_map/dot_general | solution.py:412
  285.7 5.3 %convolution_convert_fusion.2 = bf16[1152,1728]{1,0:T(8,128)(2,1)} fusion(bf16[640,1152]{1,0:T(8,128)(2,1)S(1)} %bitcast.219, bf16[640,1728]{0,1:T(8,128)(2,1)S(1)} %get-tuple-element.59), kind=kOutput, calls=%fused_computation.2 | convolution fusion | flops 2550030336 | bytes 7667712 | tf_op jit(solution)/shard_map/dot_general | solution.py:65
  291.1 6.2 %fusion.93 = f32[640,1152]{1,0:T(8,128)S(1)} fusion(bf16[640,1728]{0,1:T(8,128)(2,1)} %copy-done.58, bf16[1152,1728]{1,0:T(8,128)(2,1)} %all-gather.3.cloned.1.call-done), kind=kOutput, calls=%fused_computation.190 | convolution fusion | flops 2548039680 | bytes 9142272 | tf_op jit(solution)/shard_map/dot_general | solution.py:71
  297.3 4.4 fusion.8
  301.7 15.0 %scatter8.1 = f32[160,1152]{1,0:T(8,128)} custom-call(bf16[4,160,1152]{2,1,0:T(8,128)(2,1)} %bitcast.225), custom_call_target="tpu_custom_call" | custom-call | bytes 50400000 | tf_op jit(solution)/shard_map/scatter8/pallas_call | solution.py:295
  316.7 1.5 multiply_reduce_fusion
  320.6 13.3 %gather5.1 = bf16[4,160,1152]{2,1,0:T(8,128)(2,1)} custom-call(bf16[160,1152]{1,0:T(8,128)(2,1)} %multiply_convert_fusion.2.refs_0_), custom_call_target="tpu_custom_call" | custom-call | bytes 46800000 | tf_op jit(solution)/shard_map/gather5/pallas_call | solution.py:168
  334.0 7.1 %convolution_convert_fusion.1 = bf16[1152,1728]{1,0:T(8,128)(2,1)} fusion(bf16[640,1152]{1,0:T(8,128)(2,1)S(1)} %bitcast.224, bf16[640,1728]{0,1:T(8,128)(2,1)} %copy-done.57), kind=kOutput, calls=%fused_computation.1 | convolution fusion | flops 2550030336 | bytes 7667712 | tf_op jit(solution)/shard_map/dot_general | solution.py:65
  342.5 1.7 convolution_convert_fusion.10
  347.2 1.5 fusion.68
  353.1 1.8 fusion.7
  354.9 15.1 %scatter9.1 = f32[160,1152]{1,0:T(8,128)} custom-call(bf16[4,160,1152]{2,1,0:T(8,128)(2,1)} %bitcast.209), custom_call_target="tpu_custom_call" | custom-call | bytes 50400000 | tf_op jit(solution)/shard_map/scatter9/pallas_call | solution.py:295
  372.2 7.0 %convolution_convert_fusion = bf16[1152,1728]{0,1:T(8,128)(2,1)} fusion(bf16[640,1728]{0,1:T(8,128)(2,1)} %get-tuple-element.58, bf16[640,1152]{1,0:T(8,128)(2,1)S(1)} %bitcast.220), kind=kOutput, calls=%fused_computation | convolution fusion | flops 2550030336 | bytes 7667712 | tf_op jit(solution)/shard_map/dot_general | solution.py:65
  379.2 6.5 %copy.39 = bf16[1152,1728]{1,0:T(8,128)(2,1)} copy(bf16[1152,1728]{0,1:T(8,128)(2,1)} %convolution_convert_fusion) | data formatting | bytes 7962624 | tf_op jit(solution)/shard_map/convert_element_type | solution.py:483
  386.5 1.5 convolution_convert_fusion.8
  387.9 1.5 convolution_convert_fusion.7
  389.4 1.5 convolution_convert_fusion.6
  392.4 116.4 %scatter11.1 = (f32[144,256]{1,0:T(8,128)}, f32[144,256]{1,0:T(8,128)}, f32[16,256]{1,0:T(8,128)}, f32[144,256]{1,0:T(8,128)}, f32[144,256]{1,0:T(8,128)}, /*index=5*/f32[144,1728]{1,0:T(8,128)}) custom-call(bf16[8,144,256]{2,1,0:T(8,128)(2,1)} %bitcast.227, bf16[8,144,256]{2,1,0:T(8,128)(2,1)} %bitcast.228, bf16[8,16,256]{2,1,0:T(8,128)(2,1)} %pad.61.refs_2_, ...), custom_call_target="tpu_custom_call" | custom-call | bytes 360000000 | tf_op jit(solution)/shard_map/scatter11/pallas_call | solution.py:295
  512.7 2.1 convert_element_type.313
  514.9 2.1 convert_bitcast_fusion
  (223 shorter events, 47.6 us)
Async XLA Ops:
  7.2 61.7 %copy-start.7 = (bf16[160,1152]{1,0:T(8,128)(2,1)S(1)}, bf16[160,1152]{1,0:T(8,128)(2,1)}, u32[]{:S(2)}) copy-start(bf16[160,1152]{1,0:T(8,128)(2,1)} %param.17) | copy-start | bytes 1105924
  7.2 210.0 %all-gather.3.cloned.1.call-start = ((), (), s32[]{:S(2)}) async-start(), calls=%async_computation.2 | async-start | bytes 4644864 | tf_op jit(solution)/shard_map/all_gather | solution.py:389
  7.9 217.5 %all-gather.5.cloned.1.call-start = ((), (), s32[]{:S(2)}) async-start(), calls=%async_computation.3 | async-start | bytes 4644864 | tf_op jit(solution)/shard_map/all_gather | solution.py:390
  8.7 504.0 %reduce-scatter.3.cloned.1.call-start = ((), (), s32[]{:S(2)}) async-start(), calls=%async_computation.4 | async-start | bytes 4644864 | tf_op jit(solution)/shard_map/reduce_scatter | solution.py:486
  12.7 71.7 %copy-start.53 = (s32[640]{0:T(1024)S(1)}, s32[640]{0:T(1024)}, u32[]{:S(2)}) copy-start(s32[640]{0:T(1024)} %param.33) | copy-start | bytes 7684
  67.6 16.9 %copy-start.17 = (bf16[8,144,256]{2,1,0:T(8,128)(2,1)S(1)}, bf16[8,144,256]{2,1,0:T(8,128)(2,1)}, u32[]{:S(2)}) copy-start(bf16[8,144,256]{2,1,0:T(8,128)(2,1)} %get-tuple-element.29) | copy-start | bytes 1769476
  83.4 3.3 copy-start.1
  83.4 3.3 copy-start.15
  84.4 3.0 copy-start.49
  84.5 4.7 copy-start.51
  87.6 3.1 copy-start.48
  225.4 10.7 %copy-start.12 = (bf16[8,144,1728]{2,1,0:T(8,128)(2,1)S(1)}, bf16[8,144,1728]{2,1,0:T(8,128)(2,1)}, u32[]{:S(2)}) copy-start(bf16[8,144,1728]{2,1,0:T(8,128)(2,1)} %gather1.1) | copy-start | bytes 11943940
  236.1 4.8 copy-start.57
  240.9 16.2 %copy-start.13 = (bf16[160,1152]{1,0:T(8,128)(2,1)S(1)}, bf16[160,1152]{1,0:T(8,128)(2,1)}, u32[]{:S(2)}) copy-start(bf16[160,1152]{1,0:T(8,128)(2,1)} %param.31) | copy-start | bytes 1105924
  272.9 12.8 %copy-start.21 = (bf16[4,160,1152]{2,1,0:T(8,128)(2,1)S(1)}, bf16[4,160,1152]{2,1,0:T(8,128)(2,1)}, u32[]{:S(2)}) copy-start(bf16[4,160,1152]{2,1,0:T(8,128)(2,1)} %gather3.1) | copy-start | bytes 4423684
  291.1 223.8 %reduce-scatter.5.cloned.1.call-start = ((), (), s32[]{:S(2)}) async-start(), calls=%async_computation.5 | async-start | bytes 4644864 | tf_op jit(solution)/shard_map/reduce_scatter | solution.py:486
  291.1 6.2 %copy-start.54 = (bf16[1152,1728]{1,0:T(8,128)(2,1)S(1)}, bf16[1152,1728]{1,0:T(8,128)(2,1)}, u32[]{:S(2)}) copy-start(bf16[1152,1728]{1,0:T(8,128)(2,1)} %all-gather.5.cloned.1.call-done) | copy-start | bytes 11943940
  291.1 6.2 %copy-start.59 = (bf16[640,1728]{0,1:T(8,128)(2,1)S(1)}, bf16[640,1728]{0,1:T(8,128)(2,1)}, u32[]{:S(2)}) copy-start(bf16[640,1728]{0,1:T(8,128)(2,1)} %get-tuple-element.58) | copy-start | bytes 6635524
  301.7 16.5 %copy-start = (f32[160,1152]{1,0:T(8,128)S(1)}, f32[160,1152]{1,0:T(8,128)}, u32[]{:S(2)}) copy-start(f32[160,1152]{1,0:T(8,128)} %scatter6.1) | copy-start | bytes 2211844
  301.7 16.5 %copy-start.14 = (bf16[160,1152]{1,0:T(8,128)(2,1)S(1)}, bf16[160,1152]{1,0:T(8,128)(2,1)}, u32[]{:S(2)}) copy-start(bf16[160,1152]{1,0:T(8,128)(2,1)} %param.31) | copy-start | bytes 1105924
  320.6 13.3 %copy-start.25 = (bf16[4,160,1152]{2,1,0:T(8,128)(2,1)S(1)}, bf16[4,160,1152]{2,1,0:T(8,128)(2,1)}, u32[]{:S(2)}) copy-start(bf16[4,160,1152]{2,1,0:T(8,128)(2,1)} %gather4.1) | copy-start | bytes 4423684
  341.1 3.1 copy-start.20
  341.1 3.1 copy-start.56
  354.9 17.3 %copy-start.22 = (bf16[4,160,1152]{2,1,0:T(8,128)(2,1)S(1)}, bf16[4,160,1152]{2,1,0:T(8,128)(2,1)}, u32[]{:S(2)}) copy-start(bf16[4,160,1152]{2,1,0:T(8,128)(2,1)} %gather3.1) | copy-start | bytes 4423684
  379.2 7.2 %copy-start.29 = (bf16[640,256]{0,1:T(8,128)(2,1)S(1)}, bf16[640,256]{0,1:T(8,128)(2,1)}, u32[]{:S(2)}) copy-start(bf16[640,256]{0,1:T(8,128)(2,1)} %copy-done.28) | copy-start | bytes 983044
  392.4 119.1 %copy-start.9 = (f32[160,1152]{1,0:T(8,128)S(1)}, f32[160,1152]{1,0:T(8,128)}, u32[]{:S(2)}) copy-start(f32[160,1152]{1,0:T(8,128)} %copy-done.8) | copy-start | bytes 2211844
  392.4 119.1 %copy-start.10 = (f32[160,1152]{1,0:T(8,128)S(1)}, f32[160,1152]{1,0:T(8,128)}, u32[]{:S(2)}) copy-start(f32[160,1152]{1,0:T(8,128)} %scatter9.1) | copy-start | bytes 2211844
  512.7 4.3 copy-start.47
  512.7 5.0 copy-start.46
  512.7 5.7 %copy-start.45 = (f32[144,256]{1,0:T(8,128)S(1)}, f32[144,256]{1,0:T(8,128)}, u32[]{:S(2)}) copy-start(f32[144,256]{1,0:T(8,128)} %get-tuple-element.114) | copy-start | bytes 442372
  512.7 6.3 %copy-start.44 = (f32[144,256]{1,0:T(8,128)S(1)}, f32[144,256]{1,0:T(8,128)}, u32[]{:S(2)}) copy-start(f32[144,256]{1,0:T(8,128)} %get-tuple-element.35) | copy-start | bytes 442372
  514.8 4.8 copy-start.30
  (32 other events, 45.3 us)
Sparse Core Ops, SparseCore 0:
  10.2 94.3 all-gather.2
  106.8 103.3 all-gather.4
  291.2 88.0 reduce-scatter.2
  382.7 132.1 reduce-scatter.4
